TPU v7x, 32 devices: a whole 2x2x4 slice. The times are simulated.
32 devices in a mesh: dp: 4 (over y, x), mp: 8 (over z, core).
Axes of the slice: x: 2, y: 2, z: 4, core: 2. Of those that a mesh axis runs over, the one named last changes fastest.
Arguments:
- layer_in: bfloat16 [2048, 4, 2048], P('mp', 'dp'), may hold values from -18 to 18
- segment_ids: int32 [4, 2048], P('dp'), may hold values from 0 to 7, never falling along the last dimension, each value on 1 to 1024 neighbouring positions
- valid_counts: int32 [4], P('dp'), may hold values from 1024 to 2048
- norm_gain: float32 [2048], replicated, may hold values from 0.1 to 1.9
- norm_shift: float32 [2048], replicated, may hold values from -1.5 to 1.5
- w_qkv: bfloat16 [2048, 3, 2048], P(None, None, 'mp'), may hold values from -0.125 to 0.125
- b_qkv: bfloat16 [3, 2048], P(None, 'mp'), may hold values from -1.5 to 1.5
- w_out: bfloat16 [2048, 2048], P('mp'), may hold values from -0.5 to 0.5
- w_gate_up: bfloat16 [2048, 2, 5632], P(None, None, 'mp'), may hold values from -0.125 to 0.125
- w_down: bfloat16 [5632, 2048], P('mp'), may hold values from -0.078125 to 0.078125
- out_grad: bfloat16 [2048, 4, 2048], P('mp', 'dp'), may hold values from -6 to 6
Outputs:
- layer_out: bfloat16 [2048, 4, 2048], P('mp', 'dp')
- input_grad: float32 [2048, 4, 2048], P('mp', 'dp')
- grad_gain: float32 [2048], replicated
- grad_shift: float32 [2048], replicated
- grad_w_qkv: float32 [2048, 3, 2048], P(None, None, 'mp')
- grad_b_qkv: float32 [3, 2048], P(None, 'mp')
- grad_w_out: float32 [2048, 2048], P('mp')
- grad_w_gate_up: float32 [2048, 2, 5632], P(None, None, 'mp')
- grad_w_down: float32 [5632, 2048], P('mp')
- branch_rms: float32 [3], replicated
Inputs may be any that keep to these rules, and one draw needn't show every extreme that they name: `segment_ids`: segment ids never fall along a row; each document has 1 to 1024 tokens.
All inputs are finite; a program needn't handle non-finite values.
Results may differ from a plain program's by a relative error of at most 0.014.
Values may be sent and summed in bfloat16 or wider, within the bound.
No kernel may reach another device: no remote copies, remote signals or barrier semaphores. Data moves between devices by JAX's collectives and lax.ppermute only.
A program may use at most 256 MiB of HBM per device.

v0:
```python
import jax
import jax.numpy as jnp
from jax import lax
from jax.sharding import PartitionSpec as P

HEAD_DIM = 64
ROT = 16


EPSILON = 1e-05


def positions_of(segment_ids):
    length = segment_ids.shape[1]
    steps_all = jnp.arange(length, dtype=jnp.int32)[None, :]
    change = jnp.concatenate(
        [
            jnp.ones_like(segment_ids[:, :1]),
            (segment_ids[:, 1:] != segment_ids[:, :-1]).astype(jnp.int32),
        ],
        axis=1,
    )
    starts = lax.cummax(jnp.where(change > 0, steps_all, jnp.zeros_like(change)), axis=1)
    return steps_all - starts


def rotary_tables(positions):
    half_rot = ROT // 2
    frequency = 10000.0 ** (-(jnp.arange(half_rot, dtype=jnp.float32) * 2.0) / ROT)
    angles = positions.astype(jnp.float32)[..., None] * frequency
    return (jnp.cos(angles), jnp.sin(angles))


def rotate(values, cosine, sine_table):
    half_rot = ROT // 2
    first = values[..., :half_rot]
    second = values[..., half_rot:ROT]
    return jnp.concatenate(
        [
            first * cosine - second * sine_table,
            second * cosine + first * sine_table,
            values[..., ROT:],
        ],
        axis=-1,
    )


def rotate_back(grads, cosine, sine_table):
    half_rot = ROT // 2
    first = grads[..., :half_rot]
    second = grads[..., half_rot:ROT]
    return jnp.concatenate(
        [
            first * cosine + second * sine_table,
            second * cosine - first * sine_table,
            grads[..., ROT:],
        ],
        axis=-1,
    )


def rounded(values):
    return lax.optimization_barrier(values.astype(jnp.bfloat16)).astype(jnp.float32)


def local(
    layer_in,
    segment_ids,
    valid_counts,
    norm_gain,
    norm_shift,
    w_qkv,
    b_qkv,
    w_out,
    w_gate_up,
    w_down,
    out_grad,
):
    local_len, row_count, model_width = layer_in.shape
    seq_len = local_len * lax.axis_size("mp")
    col_qkv = w_qkv.shape[2]
    head_count = col_qkv // HEAD_DIM
    ff_local = w_gate_up.shape[2]
    score_scale = HEAD_DIM ** (-0.5)
    residual = layer_in.astype(jnp.float32)
    centered = residual - jnp.mean(residual, -1, keepdims=True)
    inv_std = lax.rsqrt(jnp.mean(centered * centered, -1, keepdims=True) + EPSILON)
    normalized = centered * inv_std
    normed = (normalized * norm_gain + norm_shift).astype(jnp.bfloat16)
    qkv_flat = w_qkv.reshape(model_width, 3 * col_qkv)
    gate_flat = w_gate_up.reshape(model_width, 2 * ff_local)
    gathered = lax.all_gather(normed, "mp", axis=0, tiled=True)
    projected = jnp.dot(gathered, qkv_flat, preferred_element_type=jnp.float32)
    gate_up = jnp.dot(gathered, gate_flat, preferred_element_type=jnp.float32)
    projected = projected + b_qkv.reshape(3 * col_qkv).astype(jnp.float32)
    cosine, sine_table = rotary_tables(positions_of(segment_ids))
    cosine = jnp.transpose(cosine, (1, 0, 2))[:, :, None, :]
    sine_table = jnp.transpose(sine_table, (1, 0, 2))[:, :, None, :]
    heads_view = projected.reshape(seq_len, row_count, 3, head_count, HEAD_DIM)
    queries = rotate(heads_view[:, :, 0], cosine, sine_table).astype(jnp.bfloat16)
    key_rows = rotate(heads_view[:, :, 1], cosine, sine_table).astype(jnp.bfloat16)
    value_rows = heads_view[:, :, 2].astype(jnp.bfloat16)
    q_heads = jnp.transpose(queries, (1, 2, 0, 3))
    k_heads = jnp.transpose(key_rows, (1, 2, 0, 3))
    v_heads = jnp.transpose(value_rows, (1, 2, 0, 3))
    block_len = min(512, seq_len)
    block_count = seq_len // block_len
    key_pos = jnp.arange(seq_len, dtype=jnp.int32)

    def scores_at(block_id):
        offset = block_id * block_len
        q_part = lax.dynamic_slice_in_dim(q_heads, offset, block_len, 2)
        logits = (
            jnp.einsum("rhqd,rhkd->rhqk", q_part, k_heads, preferred_element_type=jnp.float32)
            * score_scale
        )
        q_seg = lax.dynamic_slice_in_dim(segment_ids, offset, block_len, 1)
        q_pos = offset + jnp.arange(block_len, dtype=jnp.int32)
        allowed = (key_pos[None, None, :] <= q_pos[None, :, None]) & (
            q_seg[:, :, None] == segment_ids[:, None, :]
        )
        return (q_part, logits, allowed[:, None])

    def forward_block(block_id):
        q_part, logits, allowed = scores_at(block_id)
        masked = jnp.where(allowed, logits, -1e30)
        highest = jnp.max(masked, -1, keepdims=True)
        exponent = jnp.exp(masked - highest)
        totals = jnp.sum(exponent, -1, keepdims=True)
        weights = (exponent / totals).astype(jnp.bfloat16)
        result = jnp.einsum("rhqk,rhkd->rhqd", weights, v_heads, preferred_element_type=jnp.float32)
        return (result.astype(jnp.bfloat16), highest[..., 0] + jnp.log(totals[..., 0]))

    blocks_out, log_sums = lax.map(forward_block, jnp.arange(block_count, dtype=jnp.int32))
    attended = jnp.transpose(blocks_out, (0, 3, 1, 2, 4)).reshape(seq_len, row_count, col_qkv)
    gate_half = gate_up[..., :ff_local]
    up_half = gate_up[..., ff_local:]
    sigmoid_gate = jax.nn.sigmoid(gate_half)
    hidden = (gate_half * sigmoid_gate * up_half).astype(jnp.bfloat16)
    branches = lax.psum_scatter(
        jnp.stack(
            [
                jnp.dot(attended, w_out, preferred_element_type=jnp.float32),
                jnp.dot(hidden, w_down, preferred_element_type=jnp.float32),
            ],
            axis=2,
        ),
        "mp",
        scatter_dimension=0,
        tiled=True,
    )
    attn_part = branches[:, :, 0]
    mlp_part = branches[:, :, 1]
    layer_out = (residual + attn_part + mlp_part).astype(jnp.bfloat16)
    position_here = lax.axis_index("mp") * local_len + jnp.arange(local_len, dtype=jnp.int32)
    valid_here = (position_here[:, None] < valid_counts[None, :]).astype(jnp.float32)
    statistics = jnp.stack(
        [
            jnp.sum(valid_here * jnp.sum(residual * residual, -1)),
            jnp.sum(valid_here * jnp.sum(attn_part * attn_part, -1)),
            jnp.sum(valid_here * jnp.sum(mlp_part * mlp_part, -1)),
            jnp.sum(valid_here),
        ]
    )
    grads_full = lax.all_gather(out_grad, "mp", axis=0, tiled=True)
    valid_full = jnp.arange(seq_len, dtype=jnp.int32)[:, None] < valid_counts[None, :]
    cotangent = jnp.where(valid_full[:, :, None], grads_full, jnp.zeros_like(grads_full))
    grad_w_out = jnp.einsum("srn,srd->nd", attended, cotangent, preferred_element_type=jnp.float32)
    grad_w_down = jnp.einsum("srf,srd->fd", hidden, cotangent, preferred_element_type=jnp.float32)
    grad_att = jnp.einsum(
        "srd,nd->srn", cotangent, w_out, preferred_element_type=jnp.float32
    ).astype(jnp.bfloat16)
    grad_hid = rounded(
        jnp.einsum("srd,fd->srf", cotangent, w_down, preferred_element_type=jnp.float32)
    )
    grad_gate = grad_hid * up_half * sigmoid_gate * (1.0 + gate_half * (1.0 - sigmoid_gate))
    grad_up = grad_hid * gate_half * sigmoid_gate
    grad_gate_up = jnp.concatenate([grad_gate, grad_up], axis=-1).astype(jnp.bfloat16)
    do_heads = jnp.transpose(
        grad_att.reshape(seq_len, row_count, head_count, HEAD_DIM), (1, 2, 0, 3)
    )

    def backward_block(running, block_id):
        key_acc, value_acc = running
        q_part, logits, allowed = scores_at(block_id)
        log_total = log_sums[block_id]
        probabilities = jnp.where(allowed, jnp.exp(logits - log_total[..., None]), 0.0)
        do_part = lax.dynamic_slice_in_dim(do_heads, block_id * block_len, block_len, 2)
        grad_probs = jnp.einsum(
            "rhqd,rhkd->rhqk", do_part, v_heads, preferred_element_type=jnp.float32
        )
        inner_sum = jnp.sum(probabilities * grad_probs, -1, keepdims=True)
        grad_logits = (probabilities * (grad_probs - inner_sum)).astype(jnp.bfloat16)
        grad_query = (
            jnp.einsum("rhqk,rhkd->rhqd", grad_logits, k_heads, preferred_element_type=jnp.float32)
            * score_scale
        )
        key_acc = (
            key_acc
            + jnp.einsum("rhqk,rhqd->rhkd", grad_logits, q_part, preferred_element_type=jnp.float32)
            * score_scale
        )
        value_acc = value_acc + jnp.einsum(
            "rhqk,rhqd->rhkd",
            probabilities.astype(jnp.bfloat16),
            do_part,
            preferred_element_type=jnp.float32,
        )
        return ((key_acc, value_acc), grad_query)

    zero_acc = jnp.zeros(k_heads.shape, jnp.float32)
    (grad_keys, grad_values), grad_queries = lax.scan(
        backward_block, (zero_acc, zero_acc), jnp.arange(block_count, dtype=jnp.int32)
    )
    grad_q_rows = jnp.transpose(grad_queries, (0, 3, 1, 2, 4)).reshape(
        seq_len, row_count, head_count, HEAD_DIM
    )
    grad_k_rows = jnp.transpose(grad_keys, (2, 0, 1, 3))
    grad_v_rows = jnp.transpose(grad_values, (2, 0, 1, 3))
    grad_proj = (
        jnp.stack(
            [
                rotate_back(rounded(grad_q_rows), cosine, sine_table),
                rotate_back(rounded(grad_k_rows), cosine, sine_table),
                rounded(grad_v_rows),
            ],
            axis=2,
        )
        .reshape(seq_len, row_count, 3 * col_qkv)
        .astype(jnp.bfloat16)
    )
    grad_b_qkv = jnp.sum(grad_proj, axis=(0, 1), dtype=jnp.float32).reshape(3, col_qkv)
    grad_w_qkv = jnp.einsum("srd,srn->dn", gathered, grad_proj, preferred_element_type=jnp.float32)
    grad_w_gate_up = jnp.einsum(
        "srd,srf->df", gathered, grad_gate_up, preferred_element_type=jnp.float32
    )
    grad_normed = lax.psum_scatter(
        (
            jnp.einsum("srn,dn->srd", grad_proj, qkv_flat, preferred_element_type=jnp.float32)
            + jnp.einsum("srf,df->srd", grad_gate_up, gate_flat, preferred_element_type=jnp.float32)
        ).astype(jnp.bfloat16),
        "mp",
        scatter_dimension=0,
        tiled=True,
    ).astype(jnp.float32)
    gain_local = jnp.sum(grad_normed * normalized, axis=(0, 1))
    shift_local = jnp.sum(grad_normed, axis=(0, 1))
    grad_gain, grad_shift, totals = lax.psum((gain_local, shift_local, statistics), ("dp", "mp"))
    branch_rms = jnp.sqrt(totals[:3] / (totals[3] * model_width))
    grad_scaled = grad_normed * norm_gain
    input_grad = inv_std * (
        grad_scaled
        - jnp.mean(grad_scaled, -1, keepdims=True)
        - normalized * jnp.mean(grad_scaled * normalized, -1, keepdims=True)
    )
    input_grad = input_grad + out_grad.astype(jnp.float32) * valid_here[:, :, None]
    grad_w_qkv, grad_b_qkv, grad_w_out, grad_w_gate_up, grad_w_down = (
        lax.psum(grad_w_qkv.astype(jnp.bfloat16), "dp").astype(jnp.float32),
        lax.psum(grad_b_qkv.astype(jnp.bfloat16), "dp").astype(jnp.float32),
        lax.psum(grad_w_out.astype(jnp.bfloat16), "dp").astype(jnp.float32),
        lax.psum(grad_w_gate_up.astype(jnp.bfloat16), "dp").astype(jnp.float32),
        lax.psum(grad_w_down.astype(jnp.bfloat16), "dp").astype(jnp.float32),
    )
    return (
        layer_out,
        input_grad,
        grad_gain,
        grad_shift,
        grad_w_qkv.reshape(model_width, 3, col_qkv),
        grad_b_qkv,
        grad_w_out,
        grad_w_gate_up.reshape(model_width, 2, ff_local),
        grad_w_down,
        branch_rms,
    )


def solution(mesh):
    placed = (
        P("mp", "dp", None),
        P("dp", None),
        P("dp"),
        P(),
        P(),
        P(None, None, "mp"),
        P(None, "mp"),
        P("mp", None),
        P(None, None, "mp"),
        P("mp", None),
        P("mp", "dp", None),
    )
    return jax.shard_map(
        local,
        mesh=mesh,
        in_specs=placed,
        out_specs=(
            P("mp", "dp", None),
            P("mp", "dp", None),
            P(),
            P(),
            P(None, None, "mp"),
            P(None, "mp"),
            P("mp", None),
            P(None, None, "mp"),
            P("mp", None),
            P(),
        ),
        check_vma=False,
    )
```

profile of v0, /device:TPU:0, one launch (start us, length us, event | category | flops | bytes accessed | tf_op | source)
XLA Modules:
  0.0 1222.6 jit_solution(16023569041700593813)
XLA Ops:
  16.9 4.6 copy.23
  21.9 76.9 %all-gather.3.cloned.1.call-done = bf16[2048,1,2048]{2,0,1:T(8,128)(2,1)} async-done(((bf16[256,1,2048]{2,0,1:T(8,128)(2,1)}), bf16[2048,1,2048]{2,0,1:T(8,128)(2,1)}) %all-gather.3.cloned.1.call-update) | async-done | bytes 8388624 | tf_op jit(solution)/shard_map/all_gather | solution.py:92
  98.7 10.1 fusion.86
  112.0 68.3 %while.28 = (s32[]{:T(128)}, bf16[4,1,4,512,64]{3,4,2,1,0:T(8,128)(2,1)}, f32[4,1,4,512]{3,2,1,0:T(4,128)S(1)}, s32[4]{0:T(128)S(1)}, s32[1,2048]{1,0:T(1,128)S(...) while((s32[]{:T(128)}, ...), condition=%wide.region_7.8_spmd.clone, body=%wide.region_4.7_spmd.clone.sunk | while | flops 1127348736 | bytes 61425892 | solution.py:134
  114.2 4.6 fusion.161
  123.1 5.9 fusion.163
  140.2 5.9 fusion.163
  148.4 4.6 fusion.161
  157.3 5.9 fusion.163
  174.3 5.9 fusion.163
  180.9 7.1 fusion.99
  188.0 225.2 %while.29 = (s32[]{:T(128)}, f32[1,4,2048,64]{2,3,1,0:T(8,128)}, f32[1,4,2048,64]{2,3,1,0:T(8,128)}, bf16[4,1,4,512,64]{3,4,2,1,0:T(8,128)(2,1)}, s32[4]{0:T(128...) while((s32[]{:T(128)}, f32[1,4,2048,64]{2,3,1,0:T(8,128)}, ...), condition=%wide.region_11.12_spmd.clone, body=%wide.region_9.11_spmd.clone.sunk | while | flops 2753165824 | bytes 222898576 | solution.py:212
  205.0 5.7 copy-done.1
  210.7 6.8 fusion.175
  217.4 12.8 %multiply_reduce_fusion.4 = (f32[4,512]{1,0:T(4,128)S(1)}, f32[4,512,2048]{2,1,0:T(8,128)}) fusion(f32[4,512,2048]{2,1,0:T(8,128)} %copy-done.1, f32[4,512]{1,0:T(4,128)S(1)} %dynamic-slice_bitcast_fusion.2, pred[512,2048]{1,0:T(8,128)(4,1)S(1)} %fusion.173, bf16[1,4,2048,64]{2,3,1,0:T(8,128)(2,1)} %get-tuple-element.495, ...), kind=kOutput, calls=%fused_computation.25.clone.1 | convolution fusion | flops 557840384 | bytes 35930116 | tf_op jit(solution)/shard_map/while/body/eval_jaxpr/rhqd,rhkd->rhqk/dot_general | solution.py:189
  230.3 12.7 %multiply_convert_fusion.3 = bf16[4,512,2048]{2,1,0:T(8,128)(2,1)S(1)} fusion(f32[4,512,2048]{2,1,0:T(8,128)} %get-tuple-element.415, f32[4,512,2048]{2,1,0:T(8,128)} %copy-done.1, f32[4,512]{1,0:T(4,128)S(1)} %get-tuple-element.416, f32[4,512]{1,0:T(4,128)S(1)} %dynamic-slice_bitcast_fusion.2, pred[512,2048]{1,0:T(8,128)(4,1)S(1)} %fusion.173), kind=kLoop, calls=%fused_computation.24.clone.1 | loop fusion | flops 25165824 | bytes 43008000 | tf_op jit(solution)/shard_map/while/body/eval_jaxpr/convert_element_type | solution.py:193
  258.0 5.7 copy-done.1
  263.7 7.2 fusion.175
  270.9 12.8 %multiply_reduce_fusion.4 = (f32[4,512]{1,0:T(4,128)S(1)}, f32[4,512,2048]{2,1,0:T(8,128)}) fusion(f32[4,512,2048]{2,1,0:T(8,128)} %copy-done.1, f32[4,512]{1,0:T(4,128)S(1)} %dynamic-slice_bitcast_fusion.2, pred[512,2048]{1,0:T(8,128)(4,1)S(1)} %fusion.173, bf16[1,4,2048,64]{2,3,1,0:T(8,128)(2,1)} %get-tuple-element.495, ...), kind=kOutput, calls=%fused_computation.25.clone.1 | convolution fusion | flops 557840384 | bytes 35930116 | tf_op jit(solution)/shard_map/while/body/eval_jaxpr/rhqd,rhkd->rhqk/dot_general | solution.py:189
  283.7 12.7 %multiply_convert_fusion.3 = bf16[4,512,2048]{2,1,0:T(8,128)(2,1)S(1)} fusion(f32[4,512,2048]{2,1,0:T(8,128)} %get-tuple-element.415, f32[4,512,2048]{2,1,0:T(8,128)} %copy-done.1, f32[4,512]{1,0:T(4,128)S(1)} %get-tuple-element.416, f32[4,512]{1,0:T(4,128)S(1)} %dynamic-slice_bitcast_fusion.2, pred[512,2048]{1,0:T(8,128)(4,1)S(1)} %fusion.173), kind=kLoop, calls=%fused_computation.24.clone.1 | loop fusion | flops 25165824 | bytes 43008000 | tf_op jit(solution)/shard_map/while/body/eval_jaxpr/convert_element_type | solution.py:193
  299.1 5.0 fusion.174
  312.3 5.7 copy-done.1
  318.0 7.2 fusion.175
  325.2 12.8 %multiply_reduce_fusion.4 = (f32[4,512]{1,0:T(4,128)S(1)}, f32[4,512,2048]{2,1,0:T(8,128)}) fusion(f32[4,512,2048]{2,1,0:T(8,128)} %copy-done.1, f32[4,512]{1,0:T(4,128)S(1)} %dynamic-slice_bitcast_fusion.2, pred[512,2048]{1,0:T(8,128)(4,1)S(1)} %fusion.173, bf16[1,4,2048,64]{2,3,1,0:T(8,128)(2,1)} %get-tuple-element.495, ...), kind=kOutput, calls=%fused_computation.25.clone.1 | convolution fusion | flops 557840384 | bytes 35930116 | tf_op jit(solution)/shard_map/while/body/eval_jaxpr/rhqd,rhkd->rhqk/dot_general | solution.py:189
  338.1 12.7 %multiply_convert_fusion.3 = bf16[4,512,2048]{2,1,0:T(8,128)(2,1)S(1)} fusion(f32[4,512,2048]{2,1,0:T(8,128)} %get-tuple-element.415, f32[4,512,2048]{2,1,0:T(8,128)} %copy-done.1, f32[4,512]{1,0:T(4,128)S(1)} %get-tuple-element.416, f32[4,512]{1,0:T(4,128)S(1)} %dynamic-slice_bitcast_fusion.2, pred[512,2048]{1,0:T(8,128)(4,1)S(1)} %fusion.173), kind=kLoop, calls=%fused_computation.24.clone.1 | loop fusion | flops 25165824 | bytes 43008000 | tf_op jit(solution)/shard_map/while/body/eval_jaxpr/convert_element_type | solution.py:193
  353.5 5.0 fusion.174
  366.7 5.7 copy-done.1
  372.4 7.2 fusion.175
  379.6 12.8 %multiply_reduce_fusion.4 = (f32[4,512]{1,0:T(4,128)S(1)}, f32[4,512,2048]{2,1,0:T(8,128)}) fusion(f32[4,512,2048]{2,1,0:T(8,128)} %copy-done.1, f32[4,512]{1,0:T(4,128)S(1)} %dynamic-slice_bitcast_fusion.2, pred[512,2048]{1,0:T(8,128)(4,1)S(1)} %fusion.173, bf16[1,4,2048,64]{2,3,1,0:T(8,128)(2,1)} %get-tuple-element.495, ...), kind=kOutput, calls=%fused_computation.25.clone.1 | convolution fusion | flops 557840384 | bytes 35930116 | tf_op jit(solution)/shard_map/while/body/eval_jaxpr/rhqd,rhkd->rhqk/dot_general | solution.py:189
  392.4 12.7 %multiply_convert_fusion.3 = bf16[4,512,2048]{2,1,0:T(8,128)(2,1)S(1)} fusion(f32[4,512,2048]{2,1,0:T(8,128)} %get-tuple-element.415, f32[4,512,2048]{2,1,0:T(8,128)} %copy-done.1, f32[4,512]{1,0:T(4,128)S(1)} %get-tuple-element.416, f32[4,512]{1,0:T(4,128)S(1)} %dynamic-slice_bitcast_fusion.2, pred[512,2048]{1,0:T(8,128)(4,1)S(1)} %fusion.173), kind=kLoop, calls=%fused_computation.24.clone.1 | loop fusion | flops 25165824 | bytes 43008000 | tf_op jit(solution)/shard_map/while/body/eval_jaxpr/convert_element_type | solution.py:193
  407.8 5.0 fusion.174
  419.0 7.7 fusion.89
  433.5 8.1 fusion.77
  441.6 4.7 copy.26
  446.2 16.6 %convolution_bitcast_fusion = f32[2048,1,1408]{0,2,1:T(8,128)S(1)} fusion(bf16[2048,1408]{0,1:T(8,128)(2,1)} %bitcast.276, bf16[2048,1,2048]{2,0,1:T(8,128)(2,1)} %all-gather.3.cloned.1.call-done), kind=kOutput, calls=%fused_computation.64 | convolution fusion | flops 11811160064 | bytes 25690112 | tf_op jit(solution)/shard_map/dot_general | solution.py:94
  466.6 9.8 fusion.102
  476.4 9.8 fusion.83
  486.2 16.1 %fusion.69 = bf16[2048,1408]{0,1:T(8,128)(2,1)} fusion(bf16[2048,1,2048]{2,0,1:T(8,128)(2,1)} %all-gather.3.cloned.1.call-done, bf16[2048,704]{0,1:T(8,128)(2,1)S(1)} %get-tuple-element.267, bf16[2048,704]{0,1:T(8,128)(2,1)S(1)} %get-tuple-element.266), kind=kOutput, calls=%fused_computation.84 | convolution fusion | flops 11825577984 | bytes 19922944 | tf_op jit(solution)/shard_map/srd,srf->df/dot_general | solution.py:234
  502.3 13.0 %fusion.126 = f32[2048,2048]{1,0:T(8,128)} fusion(bf16[2048,768]{0,1:T(8,128)(2,1)} %bitcast.263, bf16[2048,768]{0,1:T(8,128)(2,1)} %bitcast.261), kind=kOutput, calls=%fused_computation.184 | convolution fusion | flops 6442450944 | bytes 23068672 | tf_op jit(solution)/shard_map/srn,dn->srd/dot_general | solution.py:239
  515.3 21.9 %fusion.53 = bf16[2048,1,2048]{2,0,1:T(8,128)(2,1)} fusion(f32[2048,2048]{1,0:T(8,128)} %fusion.126, bf16[2048,1408]{0,1:T(8,128)(2,1)} %bitcast.277, bf16[2048,704]{0,1:T(8,128)(2,1)} %copy-done.13, bf16[2048,704]{0,1:T(8,128)(2,1)} %copy-done.12), kind=kOutput, calls=%fused_computation.67 | convolution fusion | flops 11831083008 | bytes 36700160 | tf_op jit(solution)/shard_map/srf,df->srd/dot_general | solution.py:240
  541.3 10.5 convolution_bitcast_fusion.1
  551.8 18.8 %pad_maximum_fusion = f32[2048,1,2,2048]{3,0,2,1:T(8,128)} fusion(f32[2048,1,1,2048]{3,0,2,1:T(8,128)} %convolution_bitcast_fusion.1, f32[2048,1,1,2048]{3,0,2,1:T(8,128)S(1)} %convolution_bitcast_fusion.2), kind=kLoop, calls=%fused_computation.62 | loop fusion | flops 8388608 | bytes 67108864 | tf_op jit(solution)/shard_map/stack | solution.py:141
  571.4 10.1 psum.59
  582.1 162.6 %all-reduce.4.cloned.1.call-done = (bf16[2048,3,256]{2,0,1:T(8,128)(2,1)}, bf16[256,2048]{1,0:T(8,128)(2,1)}, bf16[2048,2,704]{0,2,1:T(8,128)(2,1)}, bf16[704,2048]{1,0:T(8,128)(2,1)}) async-done(((bf16[2048,3,256]{2,0,1:T(8,128)(2,1)}, bf16[256,2048]{1,0:T(8,128)(2,1)}, bf16[2048,2,704]{0,2,1:T(8,128)(2,1)}, bf16[704,2048]{1,0:T(8,128)(2,1)}), (bf16[2048,3,256]{2,0,1:T(8,128)(2,1)}, ...) | async-done | bytes 12845072 | tf_op jit(solution)/shard_map/psum | solution.py:258
  754.7 6.0 reshape.872
  760.7 75.7 %reduce-scatter.5.cloned.1.call-done = bf16[256,1,2048]{2,0,1:T(8,128)(2,1)} async-done(((bf16[2048,1,2048]{2,0,1:T(8,128)(2,1)}), bf16[256,1,2048]{2,0,1:T(8,128)(2,1)}) %reduce-scatter.5.cloned.1.call-update) | async-done | bytes 1048592 | tf_op jit(solution)/shard_map/reduce_scatter | solution.py:237
  836.4 326.2 %reduce-scatter.3.cloned.1.call-done = f32[256,1,2,2048]{3,0,2,1:T(8,128)} async-done(((f32[2048,1,2,2048]{3,0,2,1:T(8,128)}), f32[256,1,2,2048]{3,0,2,1:T(8,128)}) %reduce-scatter.3.cloned.1.call-update) | async-done | bytes 4194320 | tf_op jit(solution)/shard_map/reduce_scatter | solution.py:140
  1169.9 37.9 %all-reduce = (f32[2048]{0:T(1024)}, f32[2048]{0:T(1024)}, f32[4]{0:T(128)S(1)}) all-reduce(f32[2048]{0:T(1024)S(1)} %get-tuple-element.284, f32[2048]{0:T(1024)S(1)} %get-tuple-element.280, f32[4]{0:T(128)S(1)} %pad_maximum_fusion.5), channel_id=1, replica_groups=mesh['dp'=4,'mp'=8] {'dp','mp'}, use_global_device_ids=true, to_apply=%region_16.17 | all-reduce | flops 4100 | bytes 32800 | tf_op jit(solution)/shard_map/psum | solution.py:248
  (230 shorter events, 128.5 us)
Async XLA Ops:
  7.2 409.8 %copy-start = (bf16[704,2048]{1,0:T(8,128)(2,1)S(1)}, bf16[704,2048]{1,0:T(8,128)(2,1)}, u32[]{:S(2)}) copy-start(bf16[704,2048]{1,0:T(8,128)(2,1)} %param.24) | copy-start | bytes 8650756
  7.2 8.7 copy-start.29
  7.2 8.7 copy-start.15
  7.2 91.5 %all-gather.3.cloned.1.call-start = ((), (), s32[]{:S(2)}) async-start(), calls=%async_computation.2 | async-start | bytes 9437184 | tf_op jit(solution)/shard_map/all_gather | solution.py:92
  13.8 167.1 %all-gather.5.cloned.1.call-start = ((), (), s32[]{:S(2)}) async-start(), calls=%async_computation.4 | async-start | bytes 9437184 | tf_op jit(solution)/shard_map/all_gather | solution.py:165
  14.5 730.2 %all-reduce.4.cloned.1.call-start = ((), (), s32[]{:S(2)}) async-start(), calls=%async_computation.6 | async-start | bytes 25690112 | tf_op jit(solution)/shard_map/psum | solution.py:258
  21.8 88.6 %copy-start.19 = (f32[2048,8]{0,1:T(8,128)}, f32[2048,8]{0,1:T(8,128)S(1)}, u32[]{:S(2)}) copy-start(f32[2048,8]{0,1:T(8,128)S(1)} %get-tuple-element.289) | copy-start | bytes 196612
  21.8 88.6 %copy-start.21 = (f32[2048,8]{0,1:T(8,128)}, f32[2048,8]{0,1:T(8,128)S(1)}, u32[]{:S(2)}) copy-start(f32[2048,8]{0,1:T(8,128)S(1)} %get-tuple-element.290) | copy-start | bytes 196612
  112.0 68.8 %copy-start.30 = (pred[2048]{0:T(1024)(128)(4,1)S(1)}, pred[2048]{0:T(1024)(128)(4,1)}, u32[]{:S(2)}) copy-start(pred[2048]{0:T(1024)(128)(4,1)} %iota_compare_fusion.2) | copy-start | bytes 6148
  118.8 4.3 copy-start.3
  135.8 4.3 copy-start.3
  152.9 4.3 copy-start.3
  170.0 4.3 copy-start.3
  204.9 5.7 copy-start.1
  230.3 12.7 %copy-start.2 = (bf16[1,4,2048,64]{2,3,1,0:T(8,128)(2,1)S(1)}, bf16[1,4,2048,64]{2,3,1,0:T(8,128)(2,1)}, u32[]{:S(2)}) copy-start(bf16[1,4,2048,64]{2,3,1,0:T(8,128)(2,1)} %get-tuple-element.492) | copy-start | bytes 3145732 | tf_op jit(solution)/shard_map/while
  230.3 12.7 %copy-start.16 = (bf16[4,1,4,512,64]{3,4,2,1,0:T(8,128)(2,1)S(1)}, bf16[4,1,4,512,64]{3,4,2,1,0:T(8,128)(2,1)}, u32[]{:S(2)}) copy-start(bf16[4,1,4,512,64]{3,4,2,1,0:T(8,128)(2,1)} %get-tuple-element.472) | copy-start | bytes 3145732 | tf_op jit(solution)/shard_map/while
  245.7 4.1 copy-start.17
  258.0 5.7 copy-start.1
  283.7 12.7 %copy-start.2 = (bf16[1,4,2048,64]{2,3,1,0:T(8,128)(2,1)S(1)}, bf16[1,4,2048,64]{2,3,1,0:T(8,128)(2,1)}, u32[]{:S(2)}) copy-start(bf16[1,4,2048,64]{2,3,1,0:T(8,128)(2,1)} %get-tuple-element.492) | copy-start | bytes 3145732 | tf_op jit(solution)/shard_map/while
  283.7 12.7 %copy-start.16 = (bf16[4,1,4,512,64]{3,4,2,1,0:T(8,128)(2,1)S(1)}, bf16[4,1,4,512,64]{3,4,2,1,0:T(8,128)(2,1)}, u32[]{:S(2)}) copy-start(bf16[4,1,4,512,64]{3,4,2,1,0:T(8,128)(2,1)} %get-tuple-element.472) | copy-start | bytes 3145732 | tf_op jit(solution)/shard_map/while
  299.1 5.0 copy-start.17
  312.3 5.7 copy-start.1
  338.0 12.7 %copy-start.2 = (bf16[1,4,2048,64]{2,3,1,0:T(8,128)(2,1)S(1)}, bf16[1,4,2048,64]{2,3,1,0:T(8,128)(2,1)}, u32[]{:S(2)}) copy-start(bf16[1,4,2048,64]{2,3,1,0:T(8,128)(2,1)} %get-tuple-element.492) | copy-start | bytes 3145732 | tf_op jit(solution)/shard_map/while
  338.0 12.7 %copy-start.16 = (bf16[4,1,4,512,64]{3,4,2,1,0:T(8,128)(2,1)S(1)}, bf16[4,1,4,512,64]{3,4,2,1,0:T(8,128)(2,1)}, u32[]{:S(2)}) copy-start(bf16[4,1,4,512,64]{3,4,2,1,0:T(8,128)(2,1)} %get-tuple-element.472) | copy-start | bytes 3145732 | tf_op jit(solution)/shard_map/while
  353.5 5.0 copy-start.17
  366.7 5.7 copy-start.1
  392.4 12.7 %copy-start.2 = (bf16[1,4,2048,64]{2,3,1,0:T(8,128)(2,1)S(1)}, bf16[1,4,2048,64]{2,3,1,0:T(8,128)(2,1)}, u32[]{:S(2)}) copy-start(bf16[1,4,2048,64]{2,3,1,0:T(8,128)(2,1)} %get-tuple-element.492) | copy-start | bytes 3145732 | tf_op jit(solution)/shard_map/while
  392.4 12.7 %copy-start.16 = (bf16[4,1,4,512,64]{3,4,2,1,0:T(8,128)(2,1)S(1)}, bf16[4,1,4,512,64]{3,4,2,1,0:T(8,128)(2,1)}, u32[]{:S(2)}) copy-start(bf16[4,1,4,512,64]{3,4,2,1,0:T(8,128)(2,1)} %get-tuple-element.472) | copy-start | bytes 3145732 | tf_op jit(solution)/shard_map/while
  407.8 5.0 copy-start.17
  414.6 4.4 copy-start.32
  414.9 4.1 copy-start.31
  416.8 9.9 copy-start.4
  419.0 7.7 copy-start.18
  429.2 4.3 slice-start.4
  430.6 11.0 copy-start.6
  446.2 16.6 %copy-start.11 = (bf16[2048,1,704]{0,2,1:T(8,128)(2,1)S(1)}, bf16[2048,1,704]{0,2,1:T(8,128)(2,1)}, u32[]{:S(2)}) copy-start(bf16[2048,1,704]{0,2,1:T(8,128)(2,1)} %fusion.89) | copy-start | bytes 8650756
  466.6 9.8 copy-start.9
  466.6 19.6 %copy-start.12 = (bf16[2048,704]{0,1:T(8,128)(2,1)}, bf16[2048,704]{0,1:T(8,128)(2,1)S(1)}, u32[]{:S(2)}) copy-start(bf16[2048,704]{0,1:T(8,128)(2,1)S(1)} %get-tuple-element.266) | copy-start | bytes 8650756
  466.6 19.6 %copy-start.13 = (bf16[2048,704]{0,1:T(8,128)(2,1)}, bf16[2048,704]{0,1:T(8,128)(2,1)S(1)}, u32[]{:S(2)}) copy-start(bf16[2048,704]{0,1:T(8,128)(2,1)S(1)} %get-tuple-element.267) | copy-start | bytes 8650756
  502.3 334.2 %reduce-scatter.5.cloned.1.call-start = ((), (), s32[]{:S(2)}) async-start(), calls=%async_computation.5 | async-start | bytes 9437184 | tf_op jit(solution)/shard_map/reduce_scatter | solution.py:237
  537.1 625.5 %reduce-scatter.3.cloned.1.call-start = ((), (), s32[]{:S(2)}) async-start(), calls=%async_computation.3 | async-start | bytes 37748736 | tf_op jit(solution)/shard_map/reduce_scatter | solution.py:140
  537.2 4.1 copy-start.10
  744.7 10.0 slice-start.1
  747.7 3.7 copy-start.8
  747.7 7.1 slice-start.2
  754.7 407.9 %copy-start.23 = (f32[2048]{0:T(1024)S(1)}, f32[2048]{0:T(1024)}, u32[]{:S(2)}) copy-start(f32[2048]{0:T(1024)} %param.18) | copy-start | bytes 24580
  754.7 407.9 %copy-start.25 = (f32[256]{0:T(256)S(1)}, f32[256]{0:T(256)}, u32[]{:S(2)}) copy-start(f32[256]{0:T(256)} %copy-done.24) | copy-start | bytes 3076
  754.7 407.9 %copy-start.27 = (f32[256]{0:T(256)S(1)}, f32[256]{0:T(256)}, u32[]{:S(2)}) copy-start(f32[256]{0:T(256)} %copy-done.26) | copy-start | bytes 3076
  (10 other events, 20.1 us)
Sparse Core Ops, SparseCore 0:
  13.9 84.7 all-gather.2
  100.3 80.5 all-gather.4
  502.4 242.2 all-reduce.3
  746.9 89.5 reduce-scatter.4
  838.6 323.9 reduce-scatter.2
where the time goes:
time: 1230 us; the launch traced here: 1220 us
  waiting for transfers between devices  643 us (52%)
  matrix products  301 us (24%)
  other arithmetic  139 us (11%)
  local copies, waits for them, and re-layouts  53 us (4%)
  blocking collectives  48 us (4%)
  loops' own time  23.1 us (2%)
  between operations  15.8 us (1%)
    reduce_scatter x1, waiting for transfers between devices, local(): lax.psum_scatter(jnp.stack([jnp.dot(attended, w_out, preferred_element_ty...  326 us
    psum x1, waiting for transfers between devices, local(): lax.psum(grad_w_qkv.astype(jnp.bfloat16), 'dp').astype(jnp.float32)  163 us
    all_gather x1, waiting for transfers between devices, local(): gathered = lax.all_gather(normed, 'mp', axis=0, tiled=True)  76.9 us
    reduce_scatter x1, waiting for transfers between devices, local(): lax.psum_scatter((jnp.einsum('srn,dn->srd', grad_proj, qkv_flat, preferre...  75.7 us
    dot_general x4, matrix products, backward_block(): jnp.einsum('rhqd,rhkd->rhqk', do_part, v_heads, preferred_element_type=jn...  51.3 us
    convert_element_type x4, other arithmetic, backward_block(): (probabilities * (grad_probs - inner_sum)).astype(jnp.bfloat16)  50.8 us
    psum x1, blocking collectives, local(): lax.psum((gain_local, shift_local, statistics), ('dp', 'mp'))  37.9 us
    dot_general x8, matrix products, scores_at(): jnp.einsum('rhqd,rhkd->rhqk', q_part, k_heads, preferred_element_type=jnp...  33 us
  transfers between devices with their start and end apart: 5, of which 5 were waited for; matrix products, arithmetic and copies ran while one was open for 14% of the time, Pallas kernels for 0%

commit v1 on v0

v1 whole, which is shorter than its diff:
```python
import functools

import jax
import jax.numpy as jnp
from jax import lax
from jax.experimental import pallas as pl
from jax.experimental.pallas import tpu as pltpu
from jax.sharding import PartitionSpec as P

HEAD_DIM = 64
ROT = 16
EPSILON = 1e-05
BQ = 128
BK = 256
NEG = -1e30
F32 = jnp.float32
BF16 = jnp.bfloat16


def starts_of(segment_ids):
    length = segment_ids.shape[1]
    steps_all = jnp.arange(length, dtype=jnp.int32)[None, :]
    change = jnp.concatenate(
        [
            jnp.ones_like(segment_ids[:, :1]),
            (segment_ids[:, 1:] != segment_ids[:, :-1]).astype(jnp.int32),
        ],
        axis=1,
    )
    return lax.cummax(jnp.where(change > 0, steps_all, jnp.zeros_like(change)), axis=1)


def rotary_lanes(positions):
    half_rot = ROT // 2
    lane = jnp.arange(2 * HEAD_DIM, dtype=jnp.int32) % HEAD_DIM
    power = (lane % half_rot).astype(F32)
    frequency = jnp.where(lane < ROT, 10000.0 ** (-(power * 2.0) / ROT), 0.0)
    angles = positions.astype(F32)[:, None] * frequency
    sine = jnp.sin(angles)
    low = jnp.where(lane < half_rot, -sine, 0.0)
    high = jnp.where((lane >= half_rot) & (lane < ROT), sine, 0.0)
    return jnp.cos(angles), low, high


def lane_tile(table, columns):
    return jnp.concatenate([table] * (columns // table.shape[1]), axis=1)


def turn(values, cosine, low, high):
    columns = values.shape[1]
    half_rot = ROT // 2
    return (
        values * lane_tile(cosine, columns)
        + pltpu.roll(values, columns - half_rot, 1) * lane_tile(low, columns)
        + pltpu.roll(values, half_rot, 1) * lane_tile(high, columns)
    )


def project_kernel(x_ref, w_ref, b_ref, cos_ref, low_ref, high_ref, q_ref, k_ref, v_ref):
    columns = q_ref.shape[1]
    flat = jnp.dot(x_ref[...], w_ref[...], preferred_element_type=F32) + b_ref[...]
    tables = (cos_ref[...], low_ref[...], high_ref[...])
    queries = turn(flat[:, :columns], *tables).astype(BF16)
    q_ref[...] = (queries.astype(F32) * HEAD_DIM**-0.5).astype(BF16)
    k_ref[...] = turn(flat[:, columns : 2 * columns], *tables).astype(BF16)
    v_ref[...] = flat[:, 2 * columns :].astype(BF16)


def project(gathered, w_flat, bias, tables):
    length, width = gathered.shape
    columns = w_flat.shape[1] // 3
    rows = min(512, length)
    table_spec = pl.BlockSpec((rows, tables[0].shape[1]), lambda i: (i, 0))
    out_spec = pl.BlockSpec((rows, columns), lambda i: (i, 0))
    return pl.pallas_call(
        project_kernel,
        grid=(length // rows,),
        in_specs=[
            pl.BlockSpec((rows, width), lambda i: (i, 0)),
            pl.BlockSpec((width, 3 * columns), lambda i: (0, 0)),
            pl.BlockSpec((1, 3 * columns), lambda i: (0, 0)),
            table_spec,
            table_spec,
            table_spec,
        ],
        out_specs=[out_spec] * 3,
        out_shape=[jax.ShapeDtypeStruct((length, columns), BF16)] * 3,
        cost_estimate=pl.CostEstimate(
            flops=6 * length * width * columns,
            bytes_accessed=2 * (length * width + 3 * width * columns + 3 * length * columns),
            transcendentals=0,
        ),
        name="project",
    )(gathered, w_flat, bias, *tables)


def stack_heads(block):
    columns = block.shape[1]
    head_of = lax.broadcasted_iota(jnp.int32, block.shape, 1) // HEAD_DIM
    return jnp.concatenate(
        [
            jnp.where(head_of == head, block, jnp.zeros_like(block))
            for head in range(columns // HEAD_DIM)
        ],
        axis=0,
    )


def unstack_heads(stacked, block):
    heads = stacked.shape[1] // block
    return jnp.concatenate(
        [
            stacked[head * HEAD_DIM : (head + 1) * HEAD_DIM, head * block : (head + 1) * block]
            for head in range(heads)
        ],
        axis=0,
    ).T


def score_block(key_block, stacked_queries, key_at, start_row, query_row):
    scores = lax.dot_general(
        key_block, stacked_queries, (((1,), (1,)), ((), ())), preferred_element_type=F32
    )
    key_pos = key_at + lax.broadcasted_iota(jnp.int32, scores.shape, 0)
    allowed = (key_pos >= start_row) & (key_pos <= query_row)
    return scores, allowed


def query_rows(start_ref, block, heads):
    start_row = jnp.concatenate([start_ref[0]] * heads, axis=1)
    query_row = pl.program_id(0) * block + lax.broadcasted_iota(jnp.int32, (1, block), 1)
    return start_row, jnp.concatenate([query_row] * heads, axis=1)


def attend_kernel(first_ref, q_ref, k_ref, v_ref, start_ref, o_ref, lse_ref, acc_ref):
    block, columns = q_ref.shape
    heads = columns // HEAD_DIM
    index = pl.program_id(0)
    stacked = stack_heads(q_ref[...])
    start_row, query_row = query_rows(start_ref, block, heads)
    acc_ref[...] = jnp.zeros_like(acc_ref)

    def body(step, carry):
        highest, total = carry
        at = pl.multiple_of(step * BK, BK)
        scores, allowed = score_block(
            k_ref[pl.ds(at, BK), :], stacked, at, start_row, query_row
        )
        scores = jnp.where(allowed, scores, NEG)
        newest = jnp.maximum(highest, jnp.max(scores, axis=0, keepdims=True))
        weights = jnp.exp(scores - newest)
        scale = jnp.exp(highest - newest)
        total = total * scale + jnp.sum(weights, axis=0, keepdims=True)
        acc_ref[...] = acc_ref[...] * scale + lax.dot_general(
            v_ref[pl.ds(at, BK), :],
            weights.astype(BF16),
            (((0,), (0,)), ((), ())),
            preferred_element_type=F32,
        )
        return newest, total

    highest, total = lax.fori_loop(
        first_ref[index],
        (index * block + block - 1) // BK + 1,
        body,
        (jnp.full((1, heads * block), NEG, F32), jnp.zeros((1, heads * block), F32)),
    )
    o_ref[...] = unstack_heads(acc_ref[...] / total, block).astype(BF16)
    lse_ref[0] = highest + jnp.log(total)


def attend(first, queries, key_rows, value_rows, start_blocks):
    length, columns = queries.shape
    blocks = length // BQ
    heads = columns // HEAD_DIM
    row_spec = pl.BlockSpec((BQ, columns), lambda i, f: (i, 0))
    whole = pl.BlockSpec((length, columns), lambda i, f: (0, 0))
    return pl.pallas_call(
        attend_kernel,
        grid_spec=pltpu.PrefetchScalarGridSpec(
            num_scalar_prefetch=1,
            grid=(blocks,),
            in_specs=[
                row_spec,
                whole,
                whole,
                pl.BlockSpec((1, 1, BQ), lambda i, f: (i, 0, 0)),
            ],
            out_specs=[
                row_spec,
                pl.BlockSpec((1, 1, heads * BQ), lambda i, f: (i, 0, 0)),
            ],
            scratch_shapes=[pltpu.VMEM((columns, heads * BQ), F32)],
        ),
        out_shape=[
            jax.ShapeDtypeStruct((length, columns), BF16),
            jax.ShapeDtypeStruct((blocks, 1, heads * BQ), F32),
        ],
        cost_estimate=pl.CostEstimate(
            flops=4 * length * 1024 * columns * heads,
            bytes_accessed=8 * length * columns,
            transcendentals=length * 1024 * heads,
        ),
        name="attend",
    )(first, queries, key_rows, value_rows, start_blocks)


def attend_back_kernel(
    first_ref,
    q_ref,
    k_ref,
    v_ref,
    do_ref,
    o_ref,
    lse_ref,
    start_ref,
    cos_ref,
    low_ref,
    high_ref,
    grad_ref,
    key_acc,
    value_acc,
    query_acc,
):
    block, columns = q_ref.shape
    heads = columns // HEAD_DIM
    length = k_ref.shape[0]
    index = pl.program_id(0)

    @pl.when(index == 0)
    def _():
        key_acc[...] = jnp.zeros_like(key_acc)
        value_acc[...] = jnp.zeros_like(value_acc)

    stacked = stack_heads(q_ref[...])
    stacked_do = stack_heads(do_ref[...])
    start_row, query_row = query_rows(start_ref, block, heads)
    lse_row = lse_ref[0]
    products = do_ref[...].astype(F32) * o_ref[...].astype(F32)
    head_rows = lax.broadcasted_iota(jnp.int32, (8, columns), 0)
    head_lanes = lax.broadcasted_iota(jnp.int32, (8, columns), 1) // HEAD_DIM
    picked = lax.dot_general(
        (head_rows == head_lanes).astype(F32),
        products,
        (((1,), (1,)), ((), ())),
        precision=lax.Precision.HIGHEST,
        preferred_element_type=F32,
    )
    inner_row = jnp.concatenate([picked[head : head + 1, :] for head in range(heads)], axis=1)
    query_acc[...] = jnp.zeros_like(query_acc)

    def body(step, carry):
        at = pl.multiple_of(step * BK, BK)
        key_block = k_ref[pl.ds(at, BK), :]
        scores, allowed = score_block(key_block, stacked, at, start_row, query_row)
        weights = jnp.where(allowed, jnp.exp(scores - lse_row), 0.0)
        grad_weights = lax.dot_general(
            v_ref[pl.ds(at, BK), :],
            stacked_do,
            (((1,), (1,)), ((), ())),
            preferred_element_type=F32,
        )
        grad_scores = (weights * (grad_weights - inner_row)).astype(BF16)
        value_acc[pl.ds(at, BK), :] += jnp.dot(
            weights.astype(BF16), stacked_do, preferred_element_type=F32
        )
        key_acc[pl.ds(at, BK), :] += jnp.dot(grad_scores, stacked, preferred_element_type=F32)
        query_acc[...] += lax.dot_general(
            key_block, grad_scores, (((0,), (0,)), ((), ())), preferred_element_type=F32
        )
        return carry

    lax.fori_loop(first_ref[index], (index * block + block - 1) // BK + 1, body, 0)

    def turn_back(grads, at, rows):
        kept = grads.astype(BF16).astype(F32)
        return turn(
            kept,
            cos_ref[pl.ds(at, rows), :],
            -low_ref[pl.ds(at, rows), :],
            -high_ref[pl.ds(at, rows), :],
        ).astype(BF16)

    at_query = pl.multiple_of(index * block, block)
    grad_ref[pl.ds(at_query, block), :columns] = turn_back(
        unstack_heads(query_acc[...], block) * HEAD_DIM**-0.5, at_query, block
    )

    @pl.when(index == pl.num_programs(0) - 1)
    def _():
        def finish(step, carry):
            at = pl.multiple_of(step * BK, BK)
            grad_ref[pl.ds(at, BK), columns : 2 * columns] = turn_back(
                key_acc[pl.ds(at, BK), :], at, BK
            )
            grad_ref[pl.ds(at, BK), 2 * columns :] = value_acc[pl.ds(at, BK), :].astype(BF16)
            return carry

        lax.fori_loop(0, length // BK, finish, 0)


def attend_back(first, queries, key_rows, value_rows, grad_att, attended, lse, start_blocks, tables):
    length, columns = queries.shape
    blocks = length // BQ
    heads = columns // HEAD_DIM
    row_spec = pl.BlockSpec((BQ, columns), lambda i, f: (i, 0))
    whole = pl.BlockSpec((length, columns), lambda i, f: (0, 0))
    table_spec = pl.BlockSpec(tables[0].shape, lambda i, f: (0, 0))
    return pl.pallas_call(
        attend_back_kernel,
        grid_spec=pltpu.PrefetchScalarGridSpec(
            num_scalar_prefetch=1,
            grid=(blocks,),
            in_specs=[
                row_spec,
                whole,
                whole,
                row_spec,
                row_spec,
                pl.BlockSpec((1, 1, heads * BQ), lambda i, f: (i, 0, 0)),
                pl.BlockSpec((1, 1, BQ), lambda i, f: (i, 0, 0)),
                table_spec,
                table_spec,
                table_spec,
            ],
            out_specs=pl.BlockSpec((length, 3 * columns), lambda i, f: (0, 0)),
            scratch_shapes=[
                pltpu.VMEM((length, columns), F32),
                pltpu.VMEM((length, columns), F32),
                pltpu.VMEM((columns, heads * BQ), F32),
            ],
        ),
        out_shape=jax.ShapeDtypeStruct((length, 3 * columns), BF16),
        cost_estimate=pl.CostEstimate(
            flops=10 * length * 1024 * columns * heads,
            bytes_accessed=16 * length * columns,
            transcendentals=length * 1024 * heads,
        ),
        name="attend_back",
    )(first, queries, key_rows, value_rows, grad_att, attended, lse, start_blocks, *tables)


def bits_of(name):
    size = lax.axis_size(name)
    count = size.bit_length() - 1
    return count if size == 1 << count else None


def swap(values, name, bit):
    size = lax.axis_size(name)
    return lax.ppermute(values, name, [(i, i ^ (1 << bit)) for i in range(size)])


def sum_over_dp(grad, axis):
    count = bits_of("dp")
    if not count or grad.shape[axis] % (2 << count):
        return lax.psum(grad, "dp").astype(F32)
    mine = lax.axis_index("dp")
    done = []
    for color, half in enumerate(jnp.split(grad, 2, axis=axis)):
        order = list(range(count))
        if color:
            order.reverse()
        for bit in order:
            size = half.shape[axis] // 2
            side = (mine >> bit) & 1
            keep = lax.dynamic_slice_in_dim(half, side * size, size, axis)
            send = lax.dynamic_slice_in_dim(half, (1 - side) * size, size, axis)
            got = swap(send, "dp", bit)
            half = (keep.astype(F32) + got.astype(F32)).astype(BF16)
        for bit in reversed(order):
            side = (mine >> bit) & 1
            got = swap(half, "dp", bit)
            half = jnp.where(
                side == 0,
                jnp.concatenate([half, got], axis=axis),
                jnp.concatenate([got, half], axis=axis),
            )
        done.append(half)
    return jnp.concatenate(done, axis=axis).astype(F32)


def sum_small(values, name):
    count = bits_of(name)
    if count is None:
        return lax.psum(values, name)
    for bit in range(count):
        values = values + swap(values, name, bit)
    return values


def local(
    layer_in,
    segment_ids,
    valid_counts,
    norm_gain,
    norm_shift,
    w_qkv,
    b_qkv,
    w_out,
    w_gate_up,
    w_down,
    out_grad,
):
    local_len, row_count, model_width = layer_in.shape
    seq_len = local_len * lax.axis_size("mp")
    col_qkv = w_qkv.shape[2]
    ff_local = w_gate_up.shape[2]
    position_here = lax.axis_index("mp") * local_len + jnp.arange(local_len, dtype=jnp.int32)
    valid_here = (position_here[:, None] < valid_counts[None, :]).astype(F32)

    residual = layer_in.astype(F32)
    centered = residual - jnp.mean(residual, -1, keepdims=True)
    inv_std = lax.rsqrt(jnp.mean(centered * centered, -1, keepdims=True) + EPSILON)
    normalized = centered * inv_std
    normed = (normalized * norm_gain + norm_shift).astype(BF16)
    cot_here = jnp.where(valid_here[:, :, None] > 0, out_grad, jnp.zeros_like(out_grad))

    gathered = lax.all_gather(normed, "mp", axis=0, tiled=True)
    cot_here, gathered_first = lax.optimization_barrier((cot_here, normed))
    cotangent = lax.all_gather(cot_here, "mp", axis=0, tiled=True)

    qkv_flat = w_qkv.reshape(model_width, 3 * col_qkv)
    gate_flat = w_gate_up.reshape(model_width, 2 * ff_local)
    starts = starts_of(segment_ids)
    positions = jnp.arange(seq_len, dtype=jnp.int32)[None, :] - starts
    bias = b_qkv.reshape(1, 3 * col_qkv).astype(F32)

    def each_row(row):
        tables = rotary_lanes(positions[row])
        start_blocks = starts[row].reshape(seq_len // BQ, 1, BQ)
        first = start_blocks[:, 0, 0] // BK
        return tables, start_blocks, first

    attended_rows = []
    kept = []
    for row in range(row_count):
        tables, start_blocks, first = each_row(row)
        queries, key_rows, value_rows = project(gathered[:, row], qkv_flat, bias, tables)
        attended, lse = attend(first, queries, key_rows, value_rows, start_blocks)
        attended_rows.append(attended)
        kept.append((first, queries, key_rows, value_rows, attended, lse, start_blocks, tables))
    attended = jnp.stack(attended_rows, axis=1)

    gate_up = jnp.dot(gathered, gate_flat, preferred_element_type=F32)
    gate_half = gate_up[..., :ff_local]
    up_half = gate_up[..., ff_local:]
    sigmoid_gate = jax.nn.sigmoid(gate_half)
    hidden = (gate_half * sigmoid_gate * up_half).astype(BF16)

    def scattered(partial):
        return lax.psum_scatter(
            partial.astype(BF16), "mp", scatter_dimension=0, tiled=True
        )

    mlp_sum = scattered(jnp.dot(hidden, w_down, preferred_element_type=F32))
    attn_sum = scattered(jnp.dot(attended, w_out, preferred_element_type=F32))
    mlp_sum, attn_sum = lax.optimization_barrier((mlp_sum, attn_sum))
    mlp_part = mlp_sum.astype(F32)
    attn_part = attn_sum.astype(F32)
    layer_out = (residual + attn_part + mlp_part).astype(BF16)
    statistics = jnp.stack(
        [
            jnp.sum(valid_here * jnp.sum(residual * residual, -1)),
            jnp.sum(valid_here * jnp.sum(attn_part * attn_part, -1)),
            jnp.sum(valid_here * jnp.sum(mlp_part * mlp_part, -1)),
            jnp.sum(valid_here),
        ]
    )

    def token_sum(spec, left, right):
        return jnp.einsum(spec, left, right, preferred_element_type=F32).astype(BF16)

    grad_hid = jnp.einsum(
        "srd,fd->srf", cotangent, w_down, preferred_element_type=F32
    ).astype(BF16).astype(F32)
    grad_w_down = sum_over_dp(token_sum("srf,srd->fd", hidden, cotangent), 1)
    grad_gate = grad_hid * up_half * sigmoid_gate * (1.0 + gate_half * (1.0 - sigmoid_gate))
    grad_up = grad_hid * gate_half * sigmoid_gate
    grad_gate_up = jnp.concatenate([grad_gate, grad_up], axis=-1).astype(BF16)
    grad_w_gate_up = sum_over_dp(token_sum("srd,srf->df", gathered, grad_gate_up), 0)

    grad_att = jnp.einsum(
        "srd,nd->srn", cotangent, w_out, preferred_element_type=F32
    ).astype(BF16)
    grad_w_out = sum_over_dp(token_sum("srn,srd->nd", attended, cotangent), 1)
    grad_proj = jnp.stack(
        [
            attend_back(first, q, k, v, grad_att[:, row], att, lse, start_blocks, tables)
            for row, (first, q, k, v, att, lse, start_blocks, tables) in enumerate(kept)
        ],
        axis=1,
    )
    grad_w_qkv = sum_over_dp(token_sum("srd,srn->dn", gathered, grad_proj), 0)
    grad_normed = scattered(
        jnp.einsum("srn,dn->srd", grad_proj, qkv_flat, preferred_element_type=F32)
        + jnp.einsum("srf,df->srd", grad_gate_up, gate_flat, preferred_element_type=F32)
    ).astype(F32)

    small = jnp.concatenate(
        [
            jnp.sum(grad_normed * normalized, axis=(0, 1)),
            jnp.sum(grad_normed, axis=(0, 1)),
            statistics,
            jnp.zeros((124,), F32),
        ]
    )
    small = sum_small(sum_small(small.reshape(-1, 128), "mp"), "dp").reshape(-1)
    grad_gain = small[:model_width]
    grad_shift = small[model_width : 2 * model_width]
    totals = small[2 * model_width : 2 * model_width + 4]
    branch_rms = jnp.sqrt(totals[:3] / (totals[3] * model_width))
    grad_scaled = grad_normed * norm_gain
    input_grad = inv_std * (
        grad_scaled
        - jnp.mean(grad_scaled, -1, keepdims=True)
        - normalized * jnp.mean(grad_scaled * normalized, -1, keepdims=True)
    )
    input_grad = input_grad + cot_here.astype(F32)
    grad_b_qkv = jnp.sum(grad_proj, axis=(0, 1), dtype=F32)
    grad_b_qkv = sum_small(grad_b_qkv.reshape(-1, 128), "dp").reshape(3, col_qkv)
    return (
        layer_out,
        input_grad,
        grad_gain,
        grad_shift,
        grad_w_qkv.reshape(model_width, 3, col_qkv),
        grad_b_qkv,
        grad_w_out,
        grad_w_gate_up.reshape(model_width, 2, ff_local),
        grad_w_down,
        branch_rms,
    )


def solution(mesh):
    placed = (
        P("mp", "dp", None),
        P("dp", None),
        P("dp"),
        P(),
        P(),
        P(None, None, "mp"),
        P(None, "mp"),
        P("mp", None),
        P(None, None, "mp"),
        P("mp", None),
        P("mp", "dp", None),
    )
    return jax.shard_map(
        local,
        mesh=mesh,
        in_specs=placed,
        out_specs=(
            P("mp", "dp", None),
            P("mp", "dp", None),
            P(),
            P(),
            P(None, None, "mp"),
            P(None, "mp"),
            P("mp", None),
            P(None, None, "mp"),
            P("mp", None),
            P(),
        ),
        check_vma=False,
    )
```

time: 1230 us -> 633 us (0.51)
  waiting for transfers between devices: 643 us -> 220 us
  matrix products: 301 us -> 131 us
  Pallas kernels: 0 us -> 77.4 us
  blocking collectives: 48 us -> 0 us
  other arithmetic: 139 us -> 95.1 us
  starting transfers between devices: 0.2 us -> 37.5 us
  loops' own time: 23.1 us -> 0 us
    reduce_scatter x2 -> x3, waiting for transfers between devices: 402 us -> 0.04 us  [scattered(): lax.psum_scatter(partial.astype(BF16), 'mp', scatter_dimension=0, tiled=T...]
    dot_general x39 -> x10, matrix products: 279 us -> 110 us  [the longest x4 40.8 us: token_sum(): jnp.einsum(spec, left, right, preferred_element_type=F32).astype(BF16)]
    psum x1 -> x0, waiting for transfers between devices: 163 us -> none  [local(): lax.psum(grad_w_qkv.astype(jnp.bfloat16), 'dp').astype(jnp.float32)]
    ppermute x0 -> x39, waiting for transfers between devices: none -> 114 us  [swap(): return lax.ppermute(values, name, [(i, i ^ 1 << bit) for i in range(size)])]
    pallas_call x0 -> x3, Pallas kernels: none -> 77.4 us  [the longest x1 37.9 us: attend_back(): pl.pallas_call(attend_back_kernel, grid_spec=pltpu.PrefetchScalarGridSpec...]
    psum x2 -> x0, blocking collectives: 48 us -> none  [the longest x1 37.9 us: local(): lax.psum((gain_local, shift_local, statistics), ('dp', 'mp'))]
    select_n x1 -> x25, other arithmetic: 0.01 us -> 46.5 us  [the longest x20 37.8 us: sum_over_dp(): jnp.where(side == 0, jnp.concatenate([half, got], axis=axis), jnp.concate...]
    all_gather x1, waiting for transfers between devices: 0.56 us -> 42.6 us  [local(): cotangent = lax.all_gather(cot_here, 'mp', axis=0, tiled=True)]
  transfers between devices with their start and end apart: 5 -> 44, of which waited for: 5 -> 14; matrix products, arithmetic and copies ran while one was open for 14% -> 30% of each run, Pallas kernels for 0% -> 6%
where the time goes in v1:
time: 633 us; the launch traced here: 623 us
  waiting for transfers between devices  220 us (35%)
  matrix products  131 us (21%)
  other arithmetic  95.1 us (15%)
  Pallas kernels  77.4 us (12%)
  local copies, waits for them, and re-layouts  46.1 us (7%)
  starting transfers between devices  37.5 us (6%)
  between operations  16.1 us (3%)
    ppermute x39, waiting for transfers between devices, swap(): return lax.ppermute(values, name, [(i, i ^ 1 << bit) for i in range(size)])  114 us
    all_gather x1, waiting for transfers between devices, local(): gathered = lax.all_gather(normed, 'mp', axis=0, tiled=True)  63.3 us
    all_gather x1, waiting for transfers between devices, local(): cotangent = lax.all_gather(cot_here, 'mp', axis=0, tiled=True)  42.6 us
    dot_general x4, matrix products, token_sum(): jnp.einsum(spec, left, right, preferred_element_type=F32).astype(BF16)  40.8 us
    pallas_call x1, Pallas kernels, attend_back(): pl.pallas_call(attend_back_kernel, grid_spec=pltpu.PrefetchScalarGridSpec...  37.9 us
    select_n x20, other arithmetic, sum_over_dp(): jnp.where(side == 0, jnp.concatenate([half, got], axis=axis), jnp.concate...  37.8 us
    ppermute x39, starting transfers between devices, swap(): return lax.ppermute(values, name, [(i, i ^ 1 << bit) for i in range(size)])  37.3 us
    pallas_call x1, Pallas kernels, attend(): pl.pallas_call(attend_kernel, grid_spec=pltpu.PrefetchScalarGridSpec(num_...  27.4 us
  transfers between devices with their start and end apart: 44, of which 14 were waited for; matrix products, arithmetic and copies ran while one was open for 30% of the time, Pallas kernels for 6%

profile of v1, /device:TPU:0, one launch (start us, length us, event | category | flops | bytes accessed | tf_op | source)
XLA Modules:
  0.0 623.3 jit_solution(6821560839364427552)
XLA Ops:
  11.1 2.7 fusion.41
  15.0 2.4 broadcast_select_fusion
  18.3 4.6 copy.35
  23.0 4.9 copy.36.w_ref
  29.6 5.8 fusion.52
  35.4 63.3 %all-gather.3.cloned.1.call-done = bf16[2048,1,2048]{2,0,1:T(8,128)(2,1)} async-done(((bf16[256,1,2048]{2,0,1:T(8,128)(2,1)}), bf16[2048,1,2048]{2,0,1:T(8,128)(2,1)}) %all-gather.3.cloned.1.call-update) | async-done | bytes 8388624 | tf_op jit(solution)/shard_map/all_gather | solution.py:419
  98.7 12.1 %project.1 = (bf16[2048,256]{1,0:T(8,128)(2,1)}, bf16[2048,256]{1,0:T(8,128)(2,1)}, bf16[2048,256]{1,0:T(8,128)(2,1)}) custom-call(bf16[2048,2048]{1,0:T(8,128)(2,1)} %bitcast.126, bf16[2048,768]{1,0:T(8,128)(2,1)} %copy.36.w_ref, f32[1,768]{1,0:T(1,128)} %bitcast.124, f32[2048,128]{1,0:T(8,128)} %get-tuple-element.76.cos_ref, ...), custom_call_target="tpu_custom_call" | custom-call | flops 6442450944 | bytes 14680064 | tf_op jit(solution)/shard_map/project/pallas_call | solution.py:75
  110.8 27.4 %attend.1 = (bf16[2048,256]{1,0:T(8,128)(2,1)}, f32[16,1,512]{2,1,0:T(1,128)}) custom-call(s32[16]{0:T(128)} %and_select_fusion.2.first_ref, bf16[2048,256]{1,0:T(8,128)(2,1)} %get-tuple-element.18.q_ref, bf16[2048,256]{1,0:T(8,128)(2,1)} %get-tuple-element.19.k_ref, bf16[2048,256]{1,0:T(8,128)(2,1)} %get-tuple-element.20.v_ref, s32[16,1,128]{2,1,0:T(1,128)} %copy-done.28), custom_call_target="tpu_custom_call" | custom-call | flops 8589934592 | bytes 4194304 | tf_op jit(solution)/shard_map/attend/pallas_call | solution.py:178
  138.3 42.6 %all-gather.5.cloned.1.call-done = bf16[2048,1,2048]{2,0,1:T(8,128)(2,1)} async-done(((bf16[256,1,2048]{2,0,1:T(8,128)(2,1)}), bf16[2048,1,2048]{2,0,1:T(8,128)(2,1)}) %all-gather.5.cloned.1.call-update) | async-done | bytes 8388624 | tf_op jit(solution)/shard_map/all_gather | solution.py:421
  180.9 7.0 %fusion.30.do_ref = bf16[2048,256]{1,0:T(8,128)(2,1)} fusion(bf16[256,2048]{1,0:T(8,128)(2,1)} %param.18, bf16[2048,1,2048]{2,0,1:T(8,128)(2,1)} %all-gather.5.cloned.1.call-done), kind=kOutput, calls=%fused_computation.53 | convolution fusion | flops 2148007936 | bytes 10485760 | tf_op jit(solution)/shard_map/srd,nd->srn/dot_general | solution.py:483
  187.8 37.9 %attend_back.1 = bf16[2048,768]{1,0:T(8,128)(2,1)} custom-call(s32[16]{0:T(128)} %and_select_fusion.2.first_ref, bf16[2048,256]{1,0:T(8,128)(2,1)} %get-tuple-element.18.q_ref, bf16[2048,256]{1,0:T(8,128)(2,1)} %get-tuple-element.19.k_ref, bf16[2048,256]{1,0:T(8,128)(2,1)} %get-tuple-element.20.v_ref, bf16[2048,256]{1,0:T(8,128)(2,1)} %fusion.30.do_ref, ...), custom_call_target="tpu_custom_call" | custom-call | flops 21474836480 | bytes 8388608 | tf_op jit(solution)/shard_map/attend_back/pallas_call | solution.py:309
  225.7 12.8 %fusion.75 = f32[2048,2048]{1,0:T(8,128)} fusion(bf16[2048,768]{1,0:T(8,128)(2,1)} %attend_back.1, bf16[2048,768]{0,1:T(8,128)(2,1)} %bitcast.115), kind=kOutput, calls=%fused_computation.180 | convolution fusion | flops 6442450944 | bytes 23068672 | tf_op jit(solution)/shard_map/srn,dn->srd/dot_general | solution.py:496
  238.5 19.1 %convolution_bitcast_fusion = f32[2048,1,1408]{0,2,1:T(8,128)} fusion(bf16[2048,1408]{0,1:T(8,128)(2,1)} %bitcast.127, bf16[2048,1,2048]{2,0,1:T(8,128)(2,1)} %all-gather.3.cloned.1.call-done), kind=kOutput, calls=%fused_computation.1 | convolution fusion | flops 11811160064 | bytes 25690112 | tf_op jit(solution)/shard_map/dot_general | solution.py:445
  257.6 13.3 %fusion.29 = (bf16[2048,704]{0,1:T(8,128)(2,1)}, bf16[2048,704]{0,1:T(8,128)(2,1)}, bf16[2048,1,704]{0,2,1:T(8,128)(2,1)}) fusion(f32[2048,1,1408]{0,2,1:T(8,128)} %convolution_bitcast_fusion, bf16[704,2048]{1,0:T(8,128)(2,1)S(1)} %copy-done, bf16[2048,1,2048]{2,0,1:T(8,128)(2,1)S(1)} %bitcast.113), kind=kOutput, calls=%fused_computation.49 | convolution fusion | flops 5931532288 | bytes 31457280 | tf_op jit(solution)/shard_map/srd,fd->srf/dot_general | solution.py:474
  270.9 21.7 %fusion = bf16[2048,1,2048]{2,0,1:T(8,128)(2,1)} fusion(f32[2048,2048]{1,0:T(8,128)} %fusion.75, bf16[2048,1408]{0,1:T(8,128)(2,1)} %bitcast.128, bf16[2048,704]{0,1:T(8,128)(2,1)} %get-tuple-element.58, bf16[2048,704]{0,1:T(8,128)(2,1)} %get-tuple-element.57), kind=kOutput, calls=%fused_computation.2 | convolution fusion | flops 11831083008 | bytes 36700160 | tf_op jit(solution)/shard_map/srf,df->srd/dot_general | solution.py:497
  292.7 10.9 %convert_bitcast_fusion.1 = bf16[2048,1,2048]{2,0,1:T(8,128)(2,1)} fusion(bf16[704,2048]{1,0:T(8,128)(2,1)S(1)} %copy-done, bf16[2048,1,704]{0,2,1:T(8,128)(2,1)} %get-tuple-element.59), kind=kOutput, calls=%fused_computation.12 | convolution fusion | flops 5909774336 | bytes 14155776 | tf_op jit(solution)/shard_map/dot_general | solution.py:456
  303.7 10.7 %convolution_convert_fusion.1 = bf16[2048,768]{0,1:T(8,128)(2,1)S(1)} fusion(bf16[2048,768]{1,0:T(8,128)(2,1)} %attend_back.1, bf16[2048,1,2048]{2,0,1:T(8,128)(2,1)} %all-gather.3.cloned.1.call-done), kind=kOutput, calls=%fused_computation.30 | convolution fusion | flops 6444023808 | bytes 14680064 | tf_op jit(solution)/shard_map/srd,srn->dn/dot_general | solution.py:472
  315.7 3.9 collective-permute-start.9
  320.2 5.8 fusion.33
  332.4 5.7 convert_bitcast_fusion
  338.2 9.5 %fusion.17 = bf16[704,2048]{1,0:T(8,128)(2,1)S(1)} fusion(bf16[2048,1,2048]{2,0,1:T(8,128)(2,1)} %all-gather.5.cloned.1.call-done, bf16[2048,1,704]{0,2,1:T(8,128)(2,1)} %get-tuple-element.59), kind=kOutput, calls=%fused_computation.32 | convolution fusion | flops 5907021824 | bytes 14155776 | tf_op jit(solution)/shard_map/srf,srd->fd/dot_general | solution.py:472
  352.0 14.8 %convolution_convert_fusion = bf16[2048,1408]{0,1:T(8,128)(2,1)S(1)} fusion(bf16[2048,704]{0,1:T(8,128)(2,1)S(1)} %copy-done.37, bf16[2048,704]{0,1:T(8,128)(2,1)S(1)} %copy-done.36, bf16[2048,1,2048]{2,0,1:T(8,128)(2,1)} %all-gather.3.cloned.1.call-done), kind=kOutput, calls=%fused_computation.13 | convolution fusion | flops 11825577984 | bytes 19922944 | tf_op jit(solution)/shard_map/srd,srf->df/dot_general | solution.py:472
  375.3 16.2 %collective-permute-done.20 = bf16[256,256]{1,0:T(8,128)(2,1)S(1)} collective-permute-done((bf16[256,256]{1,0:T(8,128)(2,1)S(1)}, bf16[256,256]{1,0:T(8,128)(2,1)S(1)}, u32[]{:S(2)}, u32[]{:S(2)}) %collective-permute-start.20) | collective-permute-done | bytes 131104 | tf_op jit(solution)/shard_map/ppermute | solution.py:351
  391.7 4.8 collective-permute-done.16
  397.8 3.7 collective-permute-done.21
  409.2 29.2 %collective-permute-done.22 = bf16[256,512]{1,0:T(8,128)(2,1)S(1)} collective-permute-done((bf16[256,512]{1,0:T(8,128)(2,1)S(1)}, bf16[256,512]{1,0:T(8,128)(2,1)S(1)}, u32[]{:S(2)}, u32[]{:S(2)}) %collective-permute-start.22) | collective-permute-done | bytes 262176 | tf_op jit(solution)/shard_map/ppermute | solution.py:351
  447.1 33.7 %collective-permute-done.36 = bf16[704,256]{1,0:T(8,128)(2,1)S(1)} collective-permute-done((bf16[704,256]{1,0:T(8,128)(2,1)S(1)}, bf16[704,256]{1,0:T(8,128)(2,1)S(1)}, u32[]{:S(2)}, u32[]{:S(2)}) %collective-permute-start.36) | collective-permute-done | bytes 360480 | tf_op jit(solution)/shard_map/ppermute | solution.py:351
  484.4 4.9 collective-permute-done.10
  493.1 2.3 collective-permute-start.11
  506.2 2.4 maximum_select_fusion.15
  509.9 2.4 maximum_select_fusion.14
  515.2 2.5 maximum_select_fusion.13
  521.8 2.4 maximum_select_fusion.10
  531.9 8.7 %collective-permute-done.38 = bf16[704,512]{1,0:T(8,128)(2,1)} collective-permute-done((bf16[704,512]{1,0:T(8,128)(2,1)}, bf16[704,512]{1,0:T(8,128)(2,1)}, u32[]{:S(2)}, u32[]{:S(2)}) %collective-permute-start.38) | collective-permute-done | bytes 720928 | tf_op jit(solution)/shard_map/ppermute | solution.py:351
  546.3 3.3 maximum_convert_fusion.2
  549.6 7.9 %collective-permute-done.12 = bf16[512,768]{0,1:T(8,128)(2,1)} collective-permute-done((bf16[512,768]{0,1:T(8,128)(2,1)}, bf16[512,768]{0,1:T(8,128)(2,1)}, u32[]{:S(2)}, u32[]{:S(2)}) %collective-permute-start.12) | collective-permute-done | bytes 786464 | tf_op jit(solution)/shard_map/ppermute | solution.py:351
  562.1 2.4 maximum_select_fusion.3
  566.5 3.2 maximum_convert_fusion.1
  569.8 2.8 maximum_select_fusion.7
  573.6 3.4 maximum_select_fusion.5
  578.4 2.4 fusion.50
  580.8 5.0 fusion.46
  586.5 2.7 concatenate.194
  594.9 2.6 collective-permute-done.30
  597.5 2.7 maximum_select_fusion.1
  601.8 2.5 maximum_select_fusion
  604.8 5.9 maximum_convert_fusion
  610.7 3.5 copy.49
  (252 shorter events, 104.8 us)
Async XLA Ops:
  7.2 250.4 %copy-start = (bf16[704,2048]{1,0:T(8,128)(2,1)S(1)}, bf16[704,2048]{1,0:T(8,128)(2,1)}, u32[]{:S(2)}) copy-start(bf16[704,2048]{1,0:T(8,128)(2,1)} %param.20) | copy-start | bytes 8650756
  7.2 91.5 %all-gather.3.cloned.1.call-start = ((), (), s32[]{:S(2)}) async-start(), calls=%async_computation.3 | async-start | bytes 9437184 | tf_op jit(solution)/shard_map/all_gather | solution.py:419
  13.8 167.1 %all-gather.5.cloned.1.call-start = ((), (), s32[]{:S(2)}) async-start(), calls=%async_computation.6 | async-start | bytes 9437184 | tf_op jit(solution)/shard_map/all_gather | solution.py:421
  17.4 560.9 %reduce-scatter.8.cloned.1.call-start = ((), (), s32[]{:S(2)}) async-start(), calls=%async_computation.7 | async-start | bytes 9437184 | tf_op jit(solution)/shard_map/reduce_scatter | solution.py:452
  28.6 82.2 %copy-start.28 = (s32[16,1,128]{2,1,0:T(1,128)}, s32[16,1,128]{2,1,0:T(1,128)S(1)}, u32[]{:S(2)}) copy-start(s32[16,1,128]{2,1,0:T(1,128)S(1)} %broadcast_maximum_fusion.start_ref) | copy-start | bytes 24580
  292.6 288.1 %reduce-scatter.4.cloned.1.call-start = ((), (), s32[]{:S(2)}) async-start(), calls=%async_computation.4 | async-start | bytes 9437184 | tf_op jit(solution)/shard_map/reduce_scatter | solution.py:452
  303.6 277.2 %reduce-scatter.6.cloned.1.call-start = ((), (), s32[]{:S(2)}) async-start(), calls=%async_computation.5 | async-start | bytes 9437184 | tf_op jit(solution)/shard_map/reduce_scatter | solution.py:452
  315.7 125.1 %collective-permute-start.9 = (bf16[512,768]{0,1:T(8,128)(2,1)}, bf16[512,768]{0,1:T(8,128)(2,1)}, u32[]{:S(2)}, u32[]{:S(2)}) collective-permute-start(bf16[512,768]{0,1:T(8,128)(2,1)} %constant_dynamic-slice_fusion.13), channel_id=1, source_target_pairs={{0,16},{8,24},{16,0},{24,8},{1,17},{9,25},{17,1},{25,9},{2,18},{10... | collective-permute-start | bytes 2359304 | tf_op jit(solution)/shard_map/ppermute | solution.py:351
  320.1 51.0 %collective-permute-start.13 = (f32[6,128]{1,0:T(8,128)S(1)}, f32[6,128]{1,0:T(8,128)S(1)}, u32[]{:S(2)}, u32[]{:S(2)}) collective-permute-start(f32[6,128]{1,0:T(8,128)S(1)} %bitcast.122), channel_id=1, source_target_pairs={{0,8},{8,0},{16,24},{24,16},{1,9},{9,1},{17,25},{25,17},{2,10},{10... | collective-permute-start | bytes 9224 | tf_op jit(solution)/shard_map/ppermute | solution.py:351
  327.6 43.5 %collective-permute-start.19 = (bf16[256,512]{1,0:T(8,128)(2,1)}, bf16[256,512]{1,0:T(8,128)(2,1)}, u32[]{:S(2)}, u32[]{:S(2)}) collective-permute-start(bf16[256,512]{1,0:T(8,128)(2,1)} %constant_dynamic-slice_fusion.9), channel_id=1, source_target_pairs={{0,16},{8,24},{16,0},{24,8},{1,17},{9,25},{17,1},{25,9},{2,18},{10... | collective-permute-start | bytes 786440 | tf_op jit(solution)/shard_map/ppermute | solution.py:351
  330.4 41.9 %collective-permute-start.15 = (bf16[256,512]{1,0:T(8,128)(2,1)}, bf16[256,512]{1,0:T(8,128)(2,1)}, u32[]{:S(2)}, u32[]{:S(2)}) collective-permute-start(bf16[256,512]{1,0:T(8,128)(2,1)} %constant_dynamic-slice_fusion.11), channel_id=1, source_target_pairs={{0,8},{8,0},{16,24},{24,16},{1,9},{9,1},{17,25},{25,17},{2,10},{10... | collective-permute-start | bytes 786440 | tf_op jit(solution)/shard_map/ppermute | solution.py:351
  349.0 53.4 %collective-permute-start.35 = (bf16[704,512]{1,0:T(8,128)(2,1)}, bf16[704,512]{1,0:T(8,128)(2,1)}, u32[]{:S(2)}, u32[]{:S(2)}) collective-permute-start(bf16[704,512]{1,0:T(8,128)(2,1)} %constant_dynamic-slice_fusion.1), channel_id=1, source_target_pairs={{0,16},{8,24},{16,0},{24,8},{1,17},{9,25},{17,1},{25,9},{2,18},{10... | collective-permute-start | bytes 2162696 | tf_op jit(solution)/shard_map/ppermute | solution.py:351
  371.1 34.7 %collective-permute-start.31 = (bf16[704,512]{1,0:T(8,128)(2,1)}, bf16[704,512]{1,0:T(8,128)(2,1)}, u32[]{:S(2)}, u32[]{:S(2)}) collective-permute-start(bf16[704,512]{1,0:T(8,128)(2,1)} %constant_dynamic-slice_fusion.3), channel_id=1, source_target_pairs={{0,8},{8,0},{16,24},{24,16},{1,9},{9,1},{17,25},{25,17},{2,10},{10... | collective-permute-start | bytes 2162696 | tf_op jit(solution)/shard_map/ppermute | solution.py:351
  371.1 25.8 %collective-permute-start.14 = (f32[6,128]{1,0:T(8,128)S(1)}, f32[6,128]{1,0:T(8,128)S(1)}, u32[]{:S(2)}, u32[]{:S(2)}) collective-permute-start(f32[6,128]{1,0:T(8,128)S(1)} %bitcast_add_fusion), channel_id=1, source_target_pairs={{0,16},{8,24},{16,0},{24,8},{1,17},{9,25},{17,1},{25,9},{2,18},{10... | collective-permute-start | bytes 9224 | tf_op jit(solution)/shard_map/ppermute | solution.py:351
  372.2 19.3 %collective-permute-start.20 = (bf16[256,256]{1,0:T(8,128)(2,1)S(1)}, bf16[256,256]{1,0:T(8,128)(2,1)S(1)}, u32[]{:S(2)}, u32[]{:S(2)}) collective-permute-start(bf16[256,256]{1,0:T(8,128)(2,1)S(1)} %constant_dynamic-slice_fusion.8), channel_id=1, source_target_pairs={{0,8},{8,0},{16,24},{24,16},{1,9},{9,1},{17,25},{25,17},{2,10},{10... | collective-permute-start | bytes 393224 | tf_op jit(solution)/shard_map/ppermute | solution.py:351
  391.5 5.0 collective-permute-start.16
  396.5 5.0 collective-permute-start.21
  396.9 5.1 collective-permute-start.17
  401.5 42.8 %collective-permute-start.5 = (bf16[512,768]{0,1:T(8,128)(2,1)}, bf16[512,768]{0,1:T(8,128)(2,1)S(1)}, u32[]{:S(2)}, u32[]{:S(2)}) collective-permute-start(bf16[512,768]{0,1:T(8,128)(2,1)} %constant_dynamic-slice_fusion.15), channel_id=1, source_target_pairs={{0,8},{8,0},{16,24},{24,16},{1,9},{9,1},{17,25},{25,17},{2,10},{10... | collective-permute-start | bytes 2359304 | tf_op jit(solution)/shard_map/ppermute | solution.py:351
  401.9 95.7 %collective-permute-start.27 = (bf16[512,1408]{0,1:T(8,128)(2,1)}, bf16[512,1408]{0,1:T(8,128)(2,1)}, u32[]{:S(2)}, u32[]{:S(2)}) collective-permute-start(bf16[512,1408]{0,1:T(8,128)(2,1)} %constant_dynamic-slice_fusion.5), channel_id=1, source_target_pairs={{0,16},{8,24},{16,0},{24,8},{1,17},{9,25},{17,1},{25,9},{2,18},{10... | collective-permute-start | bytes 4325384 | tf_op jit(solution)/shard_map/ppermute | solution.py:351
  402.4 36.0 %collective-permute-start.22 = (bf16[256,512]{1,0:T(8,128)(2,1)S(1)}, bf16[256,512]{1,0:T(8,128)(2,1)S(1)}, u32[]{:S(2)}, u32[]{:S(2)}) collective-permute-start(bf16[256,512]{1,0:T(8,128)(2,1)S(1)} %maximum_select_fusion.19), channel_id=1, source_target_pairs={{0,16},{8,24},{16,0},{24,8},{1,17},{9,25},{17,1},{25,9},{2,18},{10... | collective-permute-start | bytes 786440 | tf_op jit(solution)/shard_map/ppermute | solution.py:351
  405.7 35.4 %copy-start.9 = (bf16[1024,768]{0,1:T(8,128)(2,1)S(1)}, bf16[1024,768]{0,1:T(8,128)(2,1)}, u32[]{:S(2)}) copy-start(bf16[1024,768]{0,1:T(8,128)(2,1)} %copy-done.8) | copy-start | bytes 4718596
  405.8 34.5 %collective-permute-start.18 = (bf16[256,512]{1,0:T(8,128)(2,1)S(1)}, bf16[256,512]{1,0:T(8,128)(2,1)S(1)}, u32[]{:S(2)}, u32[]{:S(2)}) collective-permute-start(bf16[256,512]{1,0:T(8,128)(2,1)S(1)} %maximum_select_fusion.18), channel_id=1, source_target_pairs={{0,8},{8,0},{16,24},{24,16},{1,9},{9,1},{17,25},{25,17},{2,10},{10... | collective-permute-start | bytes 786440 | tf_op jit(solution)/shard_map/ppermute | solution.py:351
  438.4 63.5 %collective-permute-start.23 = (bf16[512,1408]{0,1:T(8,128)(2,1)}, bf16[512,1408]{0,1:T(8,128)(2,1)}, u32[]{:S(2)}, u32[]{:S(2)}) collective-permute-start(bf16[512,1408]{0,1:T(8,128)(2,1)} %constant_dynamic-slice_fusion.7), channel_id=1, source_target_pairs={{0,8},{8,0},{16,24},{24,16},{1,9},{9,1},{17,25},{25,17},{2,10},{10... | collective-permute-start | bytes 4325384 | tf_op jit(solution)/shard_map/ppermute | solution.py:351
  440.3 40.5 %collective-permute-start.36 = (bf16[704,256]{1,0:T(8,128)(2,1)S(1)}, bf16[704,256]{1,0:T(8,128)(2,1)S(1)}, u32[]{:S(2)}, u32[]{:S(2)}) collective-permute-start(bf16[704,256]{1,0:T(8,128)(2,1)S(1)} %constant_dynamic-slice_fusion), channel_id=1, source_target_pairs={{0,8},{8,0},{16,24},{24,16},{1,9},{9,1},{17,25},{25,17},{2,10},{10... | collective-permute-start | bytes 1081352 | tf_op jit(solution)/shard_map/ppermute | solution.py:351
  440.8 41.1 %collective-permute-start.32 = (bf16[704,256]{1,0:T(8,128)(2,1)S(1)}, bf16[704,256]{1,0:T(8,128)(2,1)S(1)}, u32[]{:S(2)}, u32[]{:S(2)}) collective-permute-start(bf16[704,256]{1,0:T(8,128)(2,1)S(1)} %constant_dynamic-slice_fusion.2), channel_id=1, source_target_pairs={{0,16},{8,24},{16,0},{24,8},{1,17},{9,25},{17,1},{25,9},{2,18},{10... | collective-permute-start | bytes 1081352 | tf_op jit(solution)/shard_map/ppermute | solution.py:351
  444.3 44.9 %collective-permute-start.10 = (bf16[256,768]{0,1:T(8,128)(2,1)S(1)}, bf16[256,768]{0,1:T(8,128)(2,1)S(1)}, u32[]{:S(2)}, u32[]{:S(2)}) collective-permute-start(bf16[256,768]{0,1:T(8,128)(2,1)S(1)} %constant_dynamic-slice_fusion.12), channel_id=1, source_target_pairs={{0,8},{8,0},{16,24},{24,16},{1,9},{9,1},{17,25},{25,17},{2,10},{10... | collective-permute-start | bytes 1179656 | tf_op jit(solution)/shard_map/ppermute | solution.py:351
  446.3 43.9 %copy-start.18 = (bf16[512,768]{0,1:T(8,128)(2,1)}, bf16[512,768]{0,1:T(8,128)(2,1)S(1)}, u32[]{:S(2)}) copy-start(bf16[512,768]{0,1:T(8,128)(2,1)S(1)} %add_convert_fusion.4) | copy-start | bytes 2359300
  480.8 11.6 %collective-permute-start.6 = (bf16[256,768]{0,1:T(8,128)(2,1)}, bf16[256,768]{0,1:T(8,128)(2,1)S(1)}, u32[]{:S(2)}, u32[]{:S(2)}) collective-permute-start(bf16[256,768]{0,1:T(8,128)(2,1)} %constant_dynamic-slice_fusion.14), channel_id=1, source_target_pairs={{0,16},{8,24},{16,0},{24,8},{1,17},{9,25},{17,1},{25,9},{2,18},{10... | collective-permute-start | bytes 1179656 | tf_op jit(solution)/shard_map/ppermute | solution.py:351
  481.9 23.5 %collective-permute-start.37 = (bf16[704,256]{1,0:T(8,128)(2,1)}, bf16[704,256]{1,0:T(8,128)(2,1)}, u32[]{:S(2)}, u32[]{:S(2)}) collective-permute-start(bf16[704,256]{1,0:T(8,128)(2,1)} %add_convert_fusion.11), channel_id=1, source_target_pairs={{0,8},{8,0},{16,24},{24,16},{1,9},{9,1},{17,25},{25,17},{2,10},{10... | collective-permute-start | bytes 1081352 | tf_op jit(solution)/shard_map/ppermute | solution.py:351
  489.2 19.4 %collective-permute-start.33 = (bf16[704,256]{1,0:T(8,128)(2,1)}, bf16[704,256]{1,0:T(8,128)(2,1)}, u32[]{:S(2)}, u32[]{:S(2)}) collective-permute-start(bf16[704,256]{1,0:T(8,128)(2,1)} %add_convert_fusion.12), channel_id=1, source_target_pairs={{0,16},{8,24},{16,0},{24,8},{1,17},{9,25},{17,1},{25,9},{2,18},{10... | collective-permute-start | bytes 1081352 | tf_op jit(solution)/shard_map/ppermute | solution.py:351
  493.1 19.2 %collective-permute-start.11 = (bf16[256,768]{0,1:T(8,128)(2,1)}, bf16[256,768]{0,1:T(8,128)(2,1)}, u32[]{:S(2)}, u32[]{:S(2)}) collective-permute-start(bf16[256,768]{0,1:T(8,128)(2,1)} %add_convert_fusion.9), channel_id=1, source_target_pairs={{0,8},{8,0},{16,24},{24,16},{1,9},{9,1},{17,25},{25,17},{2,10},{10... | collective-permute-start | bytes 1179656 | tf_op jit(solution)/shard_map/ppermute | solution.py:351
  497.6 20.0 %collective-permute-start.7 = (bf16[256,768]{0,1:T(8,128)(2,1)S(1)}, bf16[256,768]{0,1:T(8,128)(2,1)}, u32[]{:S(2)}, u32[]{:S(2)}) collective-permute-start(bf16[256,768]{0,1:T(8,128)(2,1)S(1)} %add_convert_fusion.10), channel_id=1, source_target_pairs={{0,16},{8,24},{16,0},{24,8},{1,17},{9,25},{17,1},{25,9},{2,18},{10... | collective-permute-start | bytes 1179656 | tf_op jit(solution)/shard_map/ppermute | solution.py:351
  501.9 24.4 %collective-permute-start.28 = (bf16[256,1408]{0,1:T(8,128)(2,1)}, bf16[256,1408]{0,1:T(8,128)(2,1)}, u32[]{:S(2)}, u32[]{:S(2)}) collective-permute-start(bf16[256,1408]{0,1:T(8,128)(2,1)} %constant_dynamic-slice_fusion.4), channel_id=1, source_target_pairs={{0,8},{8,0},{16,24},{24,16},{1,9},{9,1},{17,25},{25,17},{2,10},{10... | collective-permute-start | bytes 2162696 | tf_op jit(solution)/shard_map/ppermute | solution.py:351
  505.5 22.2 %collective-permute-start.24 = (bf16[256,1408]{0,1:T(8,128)(2,1)}, bf16[256,1408]{0,1:T(8,128)(2,1)}, u32[]{:S(2)}, u32[]{:S(2)}) collective-permute-start(bf16[256,1408]{0,1:T(8,128)(2,1)} %constant_dynamic-slice_fusion.6), channel_id=1, source_target_pairs={{0,16},{8,24},{16,0},{24,8},{1,17},{9,25},{17,1},{25,9},{2,18},{10... | collective-permute-start | bytes 2162696 | tf_op jit(solution)/shard_map/ppermute | solution.py:351
  508.6 32.0 %collective-permute-start.38 = (bf16[704,512]{1,0:T(8,128)(2,1)}, bf16[704,512]{1,0:T(8,128)(2,1)}, u32[]{:S(2)}, u32[]{:S(2)}) collective-permute-start(bf16[704,512]{1,0:T(8,128)(2,1)} %maximum_select_fusion.15), channel_id=1, source_target_pairs={{0,16},{8,24},{16,0},{24,8},{1,17},{9,25},{17,1},{25,9},{2,18},{10... | collective-permute-start | bytes 2162696 | tf_op jit(solution)/shard_map/ppermute | solution.py:351
  512.3 31.6 %collective-permute-start.34 = (bf16[704,512]{1,0:T(8,128)(2,1)}, bf16[704,512]{1,0:T(8,128)(2,1)}, u32[]{:S(2)}, u32[]{:S(2)}) collective-permute-start(bf16[704,512]{1,0:T(8,128)(2,1)} %maximum_select_fusion.14), channel_id=1, source_target_pairs={{0,8},{8,0},{16,24},{24,16},{1,9},{9,1},{17,25},{25,17},{2,10},{10... | collective-permute-start | bytes 2162696 | tf_op jit(solution)/shard_map/ppermute | solution.py:351
  517.7 39.8 %collective-permute-start.12 = (bf16[512,768]{0,1:T(8,128)(2,1)}, bf16[512,768]{0,1:T(8,128)(2,1)}, u32[]{:S(2)}, u32[]{:S(2)}) collective-permute-start(bf16[512,768]{0,1:T(8,128)(2,1)} %maximum_select_fusion.13), channel_id=1, source_target_pairs={{0,16},{8,24},{16,0},{24,8},{1,17},{9,25},{17,1},{25,9},{2,18},{10... | collective-permute-start | bytes 2359304 | tf_op jit(solution)/shard_map/ppermute | solution.py:351
  526.3 33.4 %collective-permute-start.8 = (bf16[512,768]{0,1:T(8,128)(2,1)}, bf16[512,768]{0,1:T(8,128)(2,1)}, u32[]{:S(2)}, u32[]{:S(2)}) collective-permute-start(bf16[512,768]{0,1:T(8,128)(2,1)} %maximum_select_fusion.11), channel_id=1, source_target_pairs={{0,8},{8,0},{16,24},{24,16},{1,9},{9,1},{17,25},{25,17},{2,10},{10... | collective-permute-start | bytes 2359304 | tf_op jit(solution)/shard_map/ppermute | solution.py:351
  527.7 42.1 %collective-permute-start.29 = (bf16[256,1408]{0,1:T(8,128)(2,1)S(1)}, bf16[256,1408]{0,1:T(8,128)(2,1)}, u32[]{:S(2)}, u32[]{:S(2)}) collective-permute-start(bf16[256,1408]{0,1:T(8,128)(2,1)S(1)} %add_convert_fusion.7), channel_id=1, source_target_pairs={{0,8},{8,0},{16,24},{24,16},{1,9},{9,1},{17,25},{25,17},{2,10},{10... | collective-permute-start | bytes 2162696 | tf_op jit(solution)/shard_map/ppermute | solution.py:351
  540.6 33.0 %collective-permute-start.25 = (bf16[256,1408]{0,1:T(8,128)(2,1)}, bf16[256,1408]{0,1:T(8,128)(2,1)}, u32[]{:S(2)}, u32[]{:S(2)}) collective-permute-start(bf16[256,1408]{0,1:T(8,128)(2,1)} %add_convert_fusion.8), channel_id=1, source_target_pairs={{0,16},{8,24},{16,0},{24,8},{1,17},{9,25},{17,1},{25,9},{2,18},{10... | collective-permute-start | bytes 2162696 | tf_op jit(solution)/shard_map/ppermute | solution.py:351
  572.6 24.9 %collective-permute-start.30 = (bf16[512,1408]{0,1:T(8,128)(2,1)}, bf16[512,1408]{0,1:T(8,128)(2,1)}, u32[]{:S(2)}, u32[]{:S(2)}) collective-permute-start(bf16[512,1408]{0,1:T(8,128)(2,1)} %maximum_select_fusion.7), channel_id=1, source_target_pairs={{0,16},{8,24},{16,0},{24,8},{1,17},{9,25},{17,1},{25,9},{2,18},{10... | collective-permute-start | bytes 4325384 | tf_op jit(solution)/shard_map/ppermute | solution.py:351
  577.0 24.7 %collective-permute-start.26 = (bf16[512,1408]{0,1:T(8,128)(2,1)}, bf16[512,1408]{0,1:T(8,128)(2,1)}, u32[]{:S(2)}, u32[]{:S(2)}) collective-permute-start(bf16[512,1408]{0,1:T(8,128)(2,1)} %maximum_select_fusion.5), channel_id=1, source_target_pairs={{0,8},{8,0},{16,24},{24,16},{1,9},{9,1},{17,25},{25,17},{2,10},{10... | collective-permute-start | bytes 4325384 | tf_op jit(solution)/shard_map/ppermute | solution.py:351
  589.1 1.7 collective-permute-start
  590.8 3.8 collective-permute-start.1
  594.7 5.5 collective-permute-start.2
  600.3 4.1 collective-permute-start.3
  604.4 9.8 %collective-permute-start.4 = (f32[33,128]{1,0:T(8,128)S(1)}, f32[33,128]{1,0:T(8,128)S(1)}, u32[]{:S(2)}, u32[]{:S(2)}) collective-permute-start(f32[33,128]{1,0:T(8,128)S(1)} %add.227), channel_id=1, source_target_pairs={{0,16},{8,24},{16,0},{24,8},{1,17},{9,25},{17,1},{25,9},{2,18},{10... | collective-permute-start | bytes 50696 | tf_op jit(solution)/shard_map/ppermute | solution.py:351
  (36 other events, 297.2 us)
Sparse Core Ops, SparseCore 0:
  13.9 84.7 all-gather.2
  100.3 80.5 all-gather.4
  292.8 89.5 reduce-scatter.7
  384.5 87.9 reduce-scatter.3
  475.2 87.9 reduce-scatter.5
